TPU v7x, 32 devices: a whole 2x2x4 slice. The times are simulated.
32 devices in a mesh: row: 8 (over z, x), col: 4 (over y, core).
Axes of the slice: x: 2, y: 2, z: 4, core: 2. Of those that a mesh axis runs over, the one named last changes fastest.
Arguments:
- tokens: bfloat16 [2, 8192, 768], P(None, ('row', 'col')), may hold values from -6 to 6
- segments: int32 [2, 8192], P(None, ('row', 'col')), may hold values from 0 to 17, as said below
- positions: int32 [2, 8192], P(None, ('row', 'col')), may hold values from 0 to 799, as said below
- w_qkv: bfloat16 [768, 3, 768], P('row', None, 'col'), may hold values from -0.21875 to 0.21875
- w_out: bfloat16 [768, 768], P('col', 'row'), may hold values from -0.875 to 0.875
- w_gate_up: bfloat16 [768, 2, 3072], P('row', None, 'col'), may hold values from -0.21875 to 0.21875
- w_down: bfloat16 [3072, 768], P('col', 'row'), may hold values from -0.109375 to 0.109375
- norm_gain: bfloat16 [768, 2], P('row'), may hold values from 0.5 to 1.5
- norm_bias: bfloat16 [768, 2], P('row'), may hold values from -1.1953125 to 1.1953125
- cotangent: float32 [2, 8192, 768], P(None, ('row', 'col')), may hold values from -6 to 6
Outputs:
- layer_out: bfloat16 [2, 8192, 768], P(None, ('row', 'col'))
- input_grad: float32 [2, 8192, 768], P(None, ('row', 'col'))
- grad_qkv: float32 [768, 3, 768], P('row', None, 'col')
- grad_out: float32 [768, 768], P('col', 'row')
- grad_gate_up: float32 [768, 2, 3072], P('row', None, 'col')
- grad_down: float32 [3072, 768], P('col', 'row')
- grad_gain: float32 [768, 2], P('row')
- grad_bias: float32 [768, 2], P('row')
Inputs may be any that keep to these rules, and one draw needn't show every extreme that they name: `segments`: within each sequence documents are numbered from 0 upward and never fall; a document has at most 800 tokens and at least 60 unless it is the last of its sequence; some document has exactly 800 tokens, and in some sequence every document but the last has exactly 60 tokens. `positions`: the place of each token within its document, counted from 0.
All inputs are finite; a program needn't handle non-finite values.
Results may differ from a plain program's by a relative error of at most 0.017.
Values may be sent and summed in bfloat16 or wider, within the bound.
No kernel may reach another device: no remote copies, remote signals or barrier semaphores. Data moves between devices by JAX's collectives and lax.ppermute only.
A program may use at most 192 MiB of HBM per device.

v0:
```python
import functools
import math

import jax
import jax.numpy as jnp
from jax import lax
from jax.experimental import pallas as pl
from jax.experimental.pallas import tpu as pltpu
from jax.sharding import PartitionSpec as P

HD = 64
PAIR = 2 * HD
QROWS = 256
epsilon = 1e-12
rope_base = 1000.0
masked_score = -1e30
f32 = jnp.float32
bf16 = jnp.bfloat16

NN = (((1,), (0,)), ((), ()))
NT = (((1,), (1,)), ((), ()))
TN = (((0,), (0,)), ((), ()))


def dot(a, b, dims=NN):
    return lax.dot_general(a, b, dims, preferred_element_type=f32)


def rope_tables(positions):
    half_dim = HD // 2
    lane = jnp.arange(PAIR)
    freq = rope_base ** (-(lane % half_dim).astype(f32) / half_dim)
    sign = jnp.where(lane % HD < half_dim, -1.0, 1.0)
    angles = positions.astype(f32)[:, None] * freq[None, :]
    return jnp.cos(angles), jnp.sin(angles) * sign[None, :]


def rotated(values, cosine, sine):
    width = values.shape[1]
    cosine = jnp.concatenate([cosine] * (width // PAIR), axis=1)
    sine = jnp.concatenate([sine] * (width // PAIR), axis=1)
    lane = lax.broadcasted_iota(jnp.int32, values.shape, 1)
    up = pltpu.roll(values, width - HD // 2, 1)
    down = pltpu.roll(values, HD // 2, 1)
    return values * cosine + jnp.where(lane % HD < HD // 2, up, down) * sine


def normalize(hidden):
    centred = hidden - jnp.mean(hidden, axis=-1, keepdims=True)
    variance = jnp.mean(centred * centred, axis=-1, keepdims=True)
    inv_std = lax.rsqrt(variance + epsilon)
    return (centred * inv_std, inv_std)


def norm_back(grad_norm, normed, inv_std):
    return inv_std * (
        grad_norm
        - jnp.mean(grad_norm, axis=-1, keepdims=True)
        - normed * jnp.mean(grad_norm * normed, axis=-1, keepdims=True)
    )


BLOCKS = 4


def block_starts(width):
    return [(0, 0), (0, width // 2), (1, 0), (1, width // 2)]


def start_weights(blocks, w_ref, sems):
    @pl.when(pl.program_id(0) == 0)
    def _():
        for block, (slot, row) in zip(blocks, block_starts(w_ref.shape[1])):
            pltpu.make_async_copy(
                block, w_ref.at[slot, pl.ds(row, block.shape[0])], sems.at[slot]
            ).start()


def wait_weights(w_ref, sems, slot):
    pltpu.make_async_copy(w_ref.at[slot], w_ref.at[slot], sems.at[slot]).wait()


def weight_scratch(blocks):
    width = 2 * blocks[0].shape[0]
    return [
        pltpu.VMEM((2, width, blocks[0].shape[1]), bf16),
        pltpu.SemaphoreType.DMA((2,)),
    ]


ANY = pl.BlockSpec(memory_space=pl.ANY)


def cost(flops, nbytes, exps=0):
    return pl.CostEstimate(flops=int(flops), bytes_accessed=int(nbytes), transcendentals=int(exps))


def whole(shape):
    return pl.BlockSpec(shape, lambda *_: (0,) * len(shape), pipeline_mode=pl.Buffered(1))


def qkv_kernel(own_ref, other_ref, cos_ref, sin_ref, *rest):
    blocks, (q_ref, kv_ref, wo_ref, w_ref, sems) = rest[:BLOCKS], rest[BLOCKS:]
    slot = pl.program_id(0)
    start_weights(blocks, w_ref, sems)
    wait_weights(w_ref, sems, slot)
    part = w_ref.shape[2] // 3
    rows = own_ref.shape[0]
    for i, x_ref in enumerate((own_ref, other_ref)):
        span = slice(i * rows, (i + 1) * rows)
        cosine, sine = cos_ref[span, :], sin_ref[span, :]
        x = x_ref[...]
        q = dot(x, w_ref[slot, :, :part])
        q_ref[span, :] = (rotated(q, cosine, sine) * (1.0 / math.sqrt(HD))).astype(bf16)
        k = dot(x, w_ref[slot, :, part : 2 * part])
        kv_ref[span, :part] = rotated(k, cosine, sine).astype(bf16)
        kv_ref[span, part:] = dot(x, w_ref[slot, :, 2 * part :]).astype(bf16)
    lane = lax.broadcasted_iota(jnp.int32, (w_ref.shape[1], part), 1)
    out = jnp.zeros(lane.shape, f32)
    for h in range(3):
        piece = w_ref[slot, :, h * part : (h + 1) * part].astype(f32)
        piece = pltpu.roll(piece, (h + 1) * HD, 1)
        out = jnp.where(lane // HD == h, piece, out)
    wo_ref[...] = out.astype(bf16)


def qkv(own, other, cosine, sine, blocks):
    rows, width = own.shape
    part = blocks[0].shape[1] // 3
    table = whole((2 * rows, PAIR))
    return pl.pallas_call(
        qkv_kernel,
        grid=(2,),
        in_specs=[whole((rows, width))] * 2 + [table] * 2 + [ANY] * BLOCKS,
        out_specs=[
            pl.BlockSpec((2 * rows, part), lambda i: (0, i)),
            pl.BlockSpec((2 * rows, 2 * part), lambda i: (0, i)),
            pl.BlockSpec((width, part), lambda i: (0, i)),
        ],
        scratch_shapes=weight_scratch(blocks),
        out_shape=[
            jax.ShapeDtypeStruct((2 * rows, 2 * part), bf16),
            jax.ShapeDtypeStruct((2 * rows, 4 * part), bf16),
            jax.ShapeDtypeStruct((width, 2 * part), bf16),
        ],
        cost_estimate=cost(24 * rows * width * part, 40 * width * part),
        compiler_params=pltpu.CompilerParams(vmem_limit_bytes=12 << 20),
        name="qkv",
    )(own, other, cosine, sine, *blocks)


BITS = 5


def document_codes(segment):
    lane = jnp.arange(PAIR) % HD
    bit = (segment[:, None] >> (lane % BITS)[None, :]) & 1
    used = (lane < 2 * BITS)[None, :]
    query = jnp.where(lane[None, :] < BITS, bit, 1 - bit)
    query = jnp.where(used, query, 0).astype(bf16)
    key = jnp.where(lane[None, :] < BITS, 1 - bit, bit)
    key = jnp.where(used, key, 0).astype(f32) * -(2.0**100)
    return query, key.astype(bf16)


def coded_keys(kx_ref, kv_ref, kcode_ref):
    lane = lax.broadcasted_iota(jnp.int32, kcode_ref.shape, 1)
    for h in range(3):
        pair = slice(h // 2 * PAIR, (h // 2 + 1) * PAIR)
        kx_ref[h] = jnp.where(lane // HD == h % 2, kv_ref[:, pair], kcode_ref[...])


def attend_kernel(quarter_ref, q_ref, kv_ref, qcode_ref, kcode_ref, out_ref, log_ref, vt_ref, kx_ref, ot_ref):
    block, part = q_ref.shape
    half_of = lax.broadcasted_iota(jnp.int32, (block, PAIR), 1) // HD

    @pl.when(pl.program_id(0) == 0)
    def _():
        vt_ref[...] = kv_ref[:, part:].T
        coded_keys(kx_ref, kv_ref, kcode_ref)
        ot_ref[3 * HD :, :] = jnp.zeros((HD, block), f32)

    def head(h, _):
        pair = pl.ds(pl.multiple_of(h // 2 * PAIR, PAIR), PAIR)
        rows = pl.ds(pl.multiple_of(h * HD, HD), HD)
        coded = jnp.where(half_of == h % 2, q_ref[:, pair], qcode_ref[...])
        scores = dot(kx_ref[h], coded, NT)
        top = jnp.max(scores, axis=0, keepdims=True)
        expo = jnp.exp(scores - top)
        total = jnp.sum(expo, axis=0, keepdims=True)
        ot_ref[rows, :] = dot(vt_ref[rows, :], expo.astype(bf16)) / total
        log_ref[pl.ds(h, 1), :] = top + jnp.log(total)
        return 0

    lax.fori_loop(0, 3, head, 0)
    out_ref[...] = ot_ref[...].T.astype(bf16)


def attend(quarter, q, kv, qcode, kcode):
    rows = q.shape[0]
    part = q.shape[1] // 2
    block = rows // 2
    grid_spec = pltpu.PrefetchScalarGridSpec(
        num_scalar_prefetch=1,
        grid=(2,),
        in_specs=[
            pl.BlockSpec((block, part), lambda i, c: (i, c[0])),
            pl.BlockSpec((rows, 2 * part), lambda i, c: (0, c[0])),
            pl.BlockSpec((block, PAIR), lambda i, c: (i, 0)),
            whole((rows, PAIR)),
        ],
        out_specs=[
            pl.BlockSpec((block, part), lambda i, c: (i, 0)),
            pl.BlockSpec((8, block), lambda i, c: (0, i)),
        ],
        scratch_shapes=[
            pltpu.VMEM((part, rows), bf16),
            pltpu.VMEM((3, rows, PAIR), bf16),
            pltpu.VMEM((part, block), f32),
        ],
    )
    return pl.pallas_call(
        attend_kernel,
        grid_spec=grid_spec,
        out_shape=[
            jax.ShapeDtypeStruct((rows, part), bf16),
            jax.ShapeDtypeStruct((8, rows), f32),
        ],
        cost_estimate=cost(16 * rows * rows * part, 12 * rows * part, rows * rows * 3),
        compiler_params=pltpu.CompilerParams(vmem_limit_bytes=12 << 20),
        name="attend",
    )(quarter, q, kv, qcode, kcode)


def attend_back_kernel(
    quarter_ref, q_ref, kv_ref, own_ref, other_ref, wo_ref, att_ref, log_ref, qcode_ref, kcode_ref, cos_ref, sin_ref,
    dq_ref, dkv_ref, kt_ref, kx_ref, do_ref, delta_ref, dqt_ref, dk_ref, dv_ref,
):
    step = pl.program_id(0)
    block, part = q_ref.shape
    half_of = lax.broadcasted_iota(jnp.int32, (block, PAIR), 1) // HD

    @pl.when(step == 0)
    def _():
        kt_ref[...] = kv_ref[:, :part].T
        coded_keys(kx_ref, kv_ref, kcode_ref)
        dk_ref[...] = jnp.zeros_like(dk_ref)
        dv_ref[...] = jnp.zeros_like(dv_ref)
        dqt_ref[3 * HD :, :] = jnp.zeros((HD, block), f32)

    low = jnp.where(step < pl.num_programs(0) // 2, own_ref[...], other_ref[...])
    do = dot(low, wo_ref[...]).astype(bf16)
    do_ref[...] = do
    prod = do.astype(f32) * att_ref[...].astype(f32)
    high = prod.astype(bf16)
    rest = (prod - high.astype(f32)).astype(bf16)
    row = lax.broadcasted_iota(jnp.int32, (8, part), 0)
    lane = lax.broadcasted_iota(jnp.int32, (8, part), 1) // HD
    pick = jnp.where(row == lane, 1.0, 0.0).astype(bf16)
    delta_ref[...] = dot(pick, high, NT) + dot(pick, rest, NT)

    def head(h, _):
        pair = pl.ds(pl.multiple_of(h // 2 * PAIR, PAIR), PAIR)
        values = pl.ds(pl.multiple_of(part + h // 2 * PAIR, PAIR), PAIR)
        rows = pl.ds(pl.multiple_of(h * HD, HD), HD)
        mine = half_of == h % 2
        zero = jnp.zeros((block, PAIR), bf16)
        q = q_ref[:, pair]
        q_head = jnp.where(mine, q, zero)
        do_head = jnp.where(mine, do_ref[:, pair], zero)
        scores = dot(kx_ref[h], jnp.where(mine, q, qcode_ref[...]), NT)
        probs = jnp.exp(scores - log_ref[pl.ds(h, 1), :])
        dprobs = dot(kv_ref[:, values], do_head, NT)
        dscores = (probs * (dprobs - delta_ref[pl.ds(h, 1), :])).astype(bf16)
        dv_ref[:, pair] += dot(probs.astype(bf16), do_head)
        dk_ref[:, pair] += dot(dscores, q_head)
        dqt_ref[rows, :] = dot(kt_ref[rows, :], dscores)
        return 0

    lax.fori_loop(0, 3, head, 0)
    dq = (dqt_ref[...] * (1.0 / math.sqrt(HD))).T
    span = pl.ds(pl.multiple_of(step * block, block), block)
    dq_ref[...] = rotated(dq, cos_ref[span, :], -sin_ref[span, :]).astype(bf16)

    @pl.when(step == pl.num_programs(0) - 1)
    def _():
        dkv_ref[:, :part] = rotated(dk_ref[...], cos_ref[...], -sin_ref[...]).astype(bf16)
        dkv_ref[:, part:] = dv_ref[...].astype(bf16)


def attend_back(quarter, q, kv, own, other, wo, att, logs, qcode, kcode, cosine, sine):
    rows = q.shape[0]
    width = own.shape[1]
    part = q.shape[1] // 2
    block = rows // 2
    grid_spec = pltpu.PrefetchScalarGridSpec(
        num_scalar_prefetch=1,
        grid=(2,),
        in_specs=[
            pl.BlockSpec((block, part), lambda i, c: (i, c[0])),
            pl.BlockSpec((rows, 2 * part), lambda i, c: (0, c[0]), pipeline_mode=pl.Buffered(1)),
            whole((block, width)),
            whole((block, width)),
            pl.BlockSpec((width, part), lambda i, c: (0, c[0]), pipeline_mode=pl.Buffered(1)),
            pl.BlockSpec((block, part), lambda i, c: (i, 0)),
            pl.BlockSpec((8, block), lambda i, c: (0, i)),
            pl.BlockSpec((block, PAIR), lambda i, c: (i, 0)),
            whole((rows, PAIR)),
            whole((rows, PAIR)),
            whole((rows, PAIR)),
        ],
        out_specs=[
            pl.BlockSpec((block, part), lambda i, c: (i, 0)),
            whole((rows, 2 * part)),
        ],
        scratch_shapes=[
            pltpu.VMEM((part, rows), bf16),
            pltpu.VMEM((3, rows, PAIR), bf16),
            pltpu.VMEM((block, part), bf16),
            pltpu.VMEM((8, block), f32),
            pltpu.VMEM((part, block), f32),
            pltpu.VMEM((rows, part), f32),
            pltpu.VMEM((rows, part), f32),
        ],
    )
    return pl.pallas_call(
        attend_back_kernel,
        grid_spec=grid_spec,
        out_shape=[
            jax.ShapeDtypeStruct((rows, part), bf16),
            jax.ShapeDtypeStruct((rows, 2 * part), bf16),
        ],
        cost_estimate=cost(40 * rows * rows * part, 30 * rows * part, rows * rows * 3),
        compiler_params=pltpu.CompilerParams(vmem_limit_bytes=22 << 20),
        name="attend_back",
    )(quarter, q, kv, own, other, wo, att, logs, qcode, kcode, cosine, sine)


def project_kernel(att_a_ref, att_b_ref, wo_ref, own_ref, send_ref):
    part = att_a_ref.shape[1]
    rows = own_ref.shape[0]
    for out_ref, span in ((send_ref, slice(rows, 2 * rows)), (own_ref, slice(0, rows))):
        out = dot(att_a_ref[span, :], wo_ref[:, :part], NT) + dot(att_b_ref[span, :], wo_ref[:, part:], NT)
        out_ref[...] = out.astype(out_ref.dtype)


def project(att_a, att_b, wo):
    rows, part = att_a.shape
    rows = rows // 2
    width = wo.shape[0]
    return pl.pallas_call(
        project_kernel,
        grid=(1,),
        in_specs=[whole(att_a.shape)] * 2 + [whole(wo.shape)],
        out_specs=[whole((rows, width))] * 2,
        out_shape=[
            jax.ShapeDtypeStruct((rows, width), f32),
            jax.ShapeDtypeStruct((rows, width), bf16),
        ],
        cost_estimate=cost(8 * rows * width * part, 16 * rows * width),
        compiler_params=pltpu.CompilerParams(vmem_limit_bytes=6 << 20),
        name="project",
    )(att_a, att_b, wo)


def first_kernel(
    x_ref, own_ref, came_ref, norm_a_ref, norm_b_ref, n_ref, s_ref, low_ref, low_t_ref, gains_ref
):
    norms = jnp.concatenate([norm_a_ref[...], norm_b_ref[...]], axis=0).astype(f32).T
    gains_ref[...] = norms[:8]
    branch = own_ref[...] + came_ref[...].astype(f32)
    normed, inv = normalize(x_ref[...].astype(f32) + branch)
    n_ref[...] = normed
    s_ref[...] = jnp.broadcast_to(inv, s_ref.shape)
    first = normed * norms[0:1] + norms[2:3]
    low_ref[...] = first.astype(bf16)
    low_t_ref[...] = first.T.astype(bf16)


def first_norm(x, own, came, norm_a, norm_b):
    rows, width = x.shape
    at = norm_a.shape[1] // 128 - 1
    strip = pl.BlockSpec((width // 2, 128), lambda i: (0, at))
    return pl.pallas_call(
        first_kernel,
        grid=(1,),
        in_specs=[whole(x.shape)] * 3 + [strip] * 2,
        out_specs=[
            whole((rows, width)), whole((rows, 128)), whole((rows, width)), whole((width, rows)), whole((8, width)),
        ],
        out_shape=[
            jax.ShapeDtypeStruct((rows, width), f32),
            jax.ShapeDtypeStruct((rows, 128), f32),
            jax.ShapeDtypeStruct((rows, width), bf16),
            jax.ShapeDtypeStruct((width, rows), bf16),
            jax.ShapeDtypeStruct((8, width), f32),
        ],
        cost_estimate=cost(20 * rows * width, 16 * rows * width),
        compiler_params=pltpu.CompilerParams(vmem_limit_bytes=7 << 20),
        name="first_norm",
    )(x, own, came, norm_a, norm_b)


def mlp_kernel(has_base, low_ref, *rest):
    if has_base:
        base_ref, rest = rest[0], rest[1:]
    blocks, (act_ref, feed_ref, w_ref, sems, sum_ref) = rest[:BLOCKS], rest[BLOCKS:]
    slot = pl.program_id(0)
    half = act_ref.shape[3]
    start_weights(blocks, w_ref, sems)

    @pl.when(slot == 0)
    def _():
        sum_ref[...] = base_ref[...] if has_base else jnp.zeros_like(sum_ref)

    wait_weights(w_ref, sems, slot)

    gate = dot(low_ref[...], w_ref[slot, :, half : 2 * half])
    up = dot(low_ref[...], w_ref[slot, :, 2 * half : 3 * half])
    act_ref[0, 0] = gate.astype(bf16)
    act_ref[0, 1] = up.astype(bf16)
    act_ref[0, 2] = (gate / (1.0 + jnp.exp(-gate)) * up).astype(bf16)
    sum_ref[...] += dot(act_ref[0, 2], w_ref[slot, :, :half], NT)

    @pl.when(slot == 1)
    def _():
        feed_ref[...] = sum_ref[...].astype(feed_ref.dtype)


def mlp(low, base, blocks, half, dtype):
    rows, width = low.shape
    has_base = base is not None
    extra = [base] if has_base else []
    return pl.pallas_call(
        functools.partial(mlp_kernel, has_base),
        grid=(2,),
        in_specs=[whole((rows, width))] * (1 + has_base) + [ANY] * BLOCKS,
        out_specs=[
            pl.BlockSpec((1, 3, rows, half), lambda i: (i, 0, 0, 0)),
            whole((rows, width)),
        ],
        scratch_shapes=weight_scratch(blocks) + [pltpu.VMEM((rows, width), f32)],
        out_shape=[
            jax.ShapeDtypeStruct((2, 3, rows, half), bf16),
            jax.ShapeDtypeStruct((rows, width), dtype),
        ],
        cost_estimate=cost(12 * rows * width * half, 30 * half * width, 2 * rows * half),
        compiler_params=pltpu.CompilerParams(vmem_limit_bytes=(6 + half // 64) << 20),
        name="mlp",
    )(low, *extra, *blocks)


def second_kernel(
    n_ref, gains_ref, feed_ref, came_ref, dy_ref, out_ref, dh_ref, low_ref, low_t_ref, sums_ref
):
    first = n_ref[...] * gains_ref[0:1] + gains_ref[2:3]
    normed, inv = normalize(first + feed_ref[...] + came_ref[...].astype(f32))
    out_ref[...] = (normed * gains_ref[1:2] + gains_ref[3:4]).astype(bf16)
    dy = dy_ref[...]
    sums_ref[...] = jnp.zeros_like(sums_ref)
    sums_ref[1:2] = jnp.sum(dy * normed, axis=0, keepdims=True)
    sums_ref[3:4] = jnp.sum(dy, axis=0, keepdims=True)
    dh = norm_back(dy * gains_ref[1:2], normed, inv)
    dh_ref[...] = dh
    low_ref[...] = dh.astype(bf16)
    low_t_ref[...] = dh.T.astype(bf16)


def second_norm(n1, gains, feed, came, dy):
    rows, width = n1.shape
    full = whole((rows, width))
    return pl.pallas_call(
        second_kernel,
        grid=(1,),
        in_specs=[full, whole((8, width)), full, full, full],
        out_specs=[full, full, full, whole((width, rows)), whole((8, width))],
        out_shape=[
            jax.ShapeDtypeStruct((rows, width), bf16),
            jax.ShapeDtypeStruct((rows, width), f32),
            jax.ShapeDtypeStruct((rows, width), bf16),
            jax.ShapeDtypeStruct((width, rows), bf16),
            jax.ShapeDtypeStruct((8, width), f32),
        ],
        cost_estimate=cost(40 * rows * width, 22 * rows * width),
        compiler_params=pltpu.CompilerParams(vmem_limit_bytes=9 << 20),
        name="second_norm",
    )(n1, gains, feed, came, dy)


def mlp_back_kernel(has_base, *rest):
    dfeeds, dfeeds_t, lows_t, acts = rest[:2], rest[2:4], rest[4:6], rest[6:8]
    rest = rest[8:]
    if has_base:
        bases, rest = rest[:2], rest[2:]
    blocks, rest = rest[:BLOCKS], rest[BLOCKS:]
    own_ref, other_ref, to_x_ref, to_y_ref, keep_ref, w_ref, sems, part_ref, sum_ref = rest
    slot = pl.program_id(0)
    rows = own_ref.shape[0]
    half = acts[0].shape[3]
    start_weights(blocks, w_ref, sems)

    @pl.when(slot == 0)
    def _():
        for i in range(2):
            sum_ref[i * rows : (i + 1) * rows, :] = (
                bases[i][...] if has_base else jnp.zeros((rows, sum_ref.shape[1]), f32)
            )

    wait_weights(w_ref, sems, slot)

    for i in range(2):
        span = slice(i * rows, (i + 1) * rows)
        dhidden = dot(dfeeds[i][...], w_ref[slot, :, :half])
        gate = acts[i][0, 0].astype(f32)
        up = acts[i][0, 1].astype(f32)
        sg = 1.0 / (1.0 + jnp.exp(-gate))
        dgate = dhidden * up * sg * (1.0 + gate * (1.0 - sg))
        dup = dhidden * (gate * sg)
        part_ref[span, :half] = dgate.astype(bf16)
        part_ref[span, half:] = dup.astype(bf16)
        sum_ref[span, :] += dot(part_ref[span, :], w_ref[slot, :, half : 3 * half], NT)
    gate_up = (
        dot(lows_t[0][...], part_ref[:rows, :]) + dot(lows_t[1][...], part_ref[rows:, :])
    ).astype(bf16)
    down = (
        dot(dfeeds_t[0][...], acts[0][0, 2]) + dot(dfeeds_t[1][...], acts[1][0, 2])
    ).astype(bf16)
    cut = keep_ref.shape[1]

    def emit(out_ref, at, block):
        span = slice(block * cut, (block + 1) * cut)
        out_ref[at, :, :half] = down[span]
        out_ref[at, :, half:] = gate_up[span]

    emit(to_x_ref, 0, 3)

    @pl.when(slot == 0)
    def _():
        for block in range(3):
            emit(keep_ref, block, block)

    @pl.when(slot == 1)
    def _():
        emit(to_y_ref, 0, 0)
        emit(to_y_ref, 1, 2)
        emit(keep_ref, 3, 1)
        own_ref[...] = sum_ref[:rows, :]
        other_ref[...] = sum_ref[rows:, :].astype(other_ref.dtype)


def mlp_back(bases, dfeeds, dfeeds_t, lows_t, acts, blocks):
    rows, width = dfeeds[0].shape
    half = acts[0].shape[3]
    has_base = bases is not None
    full = whole((rows, width))
    return pl.pallas_call(
        functools.partial(mlp_back_kernel, has_base),
        grid=(2,),
        in_specs=[full] * 2
        + [whole((width, rows))] * 4
        + [pl.BlockSpec((1, 3, rows, half), lambda i: (i, 0, 0, 0))] * 2
        + [full] * (2 * has_base)
        + [ANY] * BLOCKS,
        out_specs=[
            full,
            full,
            pl.BlockSpec((1, width // 4, 3 * half), lambda i: (i, 0, 0)),
            whole((2, width // 4, 3 * half)),
            whole((4, width // 4, 3 * half)),
        ],
        scratch_shapes=weight_scratch(blocks)
        + [pltpu.VMEM((2 * rows, 2 * half), bf16), pltpu.VMEM((2 * rows, width), f32)],
        out_shape=[
            jax.ShapeDtypeStruct((rows, width), f32),
            jax.ShapeDtypeStruct((rows, width), bf16 if has_base else f32),
            jax.ShapeDtypeStruct((2, width // 4, 3 * half), bf16),
            jax.ShapeDtypeStruct((2, width // 4, 3 * half), bf16),
            jax.ShapeDtypeStruct((4, width // 4, 3 * half), bf16),
        ],
        cost_estimate=cost(48 * rows * width * half, 100 * half * width, 4 * rows * half),
        compiler_params=pltpu.CompilerParams(vmem_limit_bytes=(5 + half // 28) << 20),
        name="mlp_back",
    )(*dfeeds, *dfeeds_t, *lows_t, *acts, *(bases if has_base else ()), *blocks)


def first_back_kernel(
    base_ref, own_ref, came_ref, n_ref, s_ref, gains_ref, sums_ref, dh_ref, low_ref, low_t_ref
):
    dfirst = base_ref[...] + own_ref[...] + came_ref[...].astype(f32)
    normed = n_ref[...]
    width = dfirst.shape[1]
    gain_sum = jnp.sum(dfirst * normed, axis=0, keepdims=True)
    bias_sum = jnp.sum(dfirst, axis=0, keepdims=True)
    sums = sums_ref[...]
    stacked = jnp.concatenate(
        [gain_sum, sums[1:2], bias_sum, sums[3:4], jnp.zeros((124, width), f32)], axis=0
    )
    rows = dfirst.shape[0]
    low_t_ref[:, rows:] = stacked.T.astype(bf16)
    dh = norm_back(dfirst * gains_ref[0:1], normed, s_ref[:, 0:1])
    dh_ref[...] = dh
    low_ref[...] = dh.astype(bf16)
    low_t_ref[:, :rows] = dh.T.astype(bf16)


def first_back(base, own, came, n1, s1, gains, sums):
    rows, width = n1.shape
    full = whole((rows, width))
    return pl.pallas_call(
        first_back_kernel,
        grid=(1,),
        in_specs=[full] * 4 + [whole((rows, 128)), whole((8, width)), whole((8, width))],
        out_specs=[full, full, whole((width, rows + 128))],
        out_shape=[
            jax.ShapeDtypeStruct((rows, width), f32),
            jax.ShapeDtypeStruct((rows, width), bf16),
            jax.ShapeDtypeStruct((width, rows + 128), bf16),
        ],
        cost_estimate=cost(40 * rows * width, 20 * rows * width),
        compiler_params=pltpu.CompilerParams(vmem_limit_bytes=9 << 20),
        name="first_back",
    )(base, own, came, n1, s1, gains, sums)


def qkv_back_kernel(
    dq_ref, dkv_ref, x_a_ref, x_b_ref, low_a_ref, low_b_ref, cols_a_ref, cols_b_ref, att_ref, base_own_ref, base_other_ref,
    top_ref, bottom_ref, own_ref, other_ref, early_ref, mid_ref, late_ref, w_ref, sem,
):
    rows = own_ref.shape[0]
    part = dq_ref.shape[1]
    copies = [
        pltpu.make_async_copy(top_ref, w_ref.at[pl.ds(0, top_ref.shape[0])], sem),
        pltpu.make_async_copy(bottom_ref, w_ref.at[pl.ds(top_ref.shape[0], top_ref.shape[0])], sem),
    ]
    for copy in copies:
        copy.start()
    d_out = dot(low_a_ref[...], att_ref[:rows, :]) + dot(low_b_ref[...], att_ref[rows:, :])
    lane = lax.broadcasted_iota(jnp.int32, d_out.shape, 1)
    cut = mid_ref.shape[0]

    def emit(value, lanes):
        early_ref[0, :, lanes] = value[:cut]
        mid_ref[:, lanes] = value[cut : 2 * cut]
        early_ref[1, :, lanes] = value[2 * cut : 3 * cut]
        late_ref[:, lanes] = value[3 * cut :]

    for h in range(3):
        source, at = (dq_ref, 0) if h == 0 else (dkv_ref, (h - 1) * part)
        piece = dot(x_a_ref[...], source[:rows, at : at + part]) + dot(x_b_ref[...], source[rows:, at : at + part])
        moved = pltpu.roll(d_out, (3 - h) * HD, 1)
        emit(jnp.where(lane < 3 * HD, piece, moved).astype(bf16), slice(h * part, (h + 1) * part))
    cols = cols_a_ref[...].astype(f32) + cols_b_ref[...].astype(f32)
    emit(cols.astype(bf16), slice(3 * part, 3 * part + 128))
    pltpu.make_async_copy(w_ref, w_ref, sem).wait()
    for i, (base_ref, out_ref) in enumerate(((base_own_ref, own_ref), (base_other_ref, other_ref))):
        span = slice(i * rows, (i + 1) * rows)
        total = dot(dq_ref[span, :], w_ref[:, :part], NT) + dot(dkv_ref[span, :], w_ref[:, part:], NT)
        out_ref[...] = (total + base_ref[...].astype(f32)).astype(out_ref.dtype)


def qkv_back(bases, dq, dkv, x_t, low_t, att, blocks):
    rows = dq.shape[0] // 2
    width = low_t[0].shape[0]
    part = dq.shape[1]
    lanes = 3 * part + 128
    full = whole((rows, width))
    turned = whole((width, rows))
    strip = pl.BlockSpec((width, 128), lambda i: (0, rows // 128), pipeline_mode=pl.Buffered(1))
    pieces = [(2, width // 4, lanes), (width // 4, lanes), (width // 4, lanes)]
    return pl.pallas_call(
        qkv_back_kernel,
        grid=(1,),
        in_specs=[whole(dq.shape), whole(dkv.shape)]
        + [turned] * 4
        + [strip] * 2
        + [whole(att.shape), full, full, ANY, ANY],
        out_specs=[full, full] + [whole(p) for p in pieces],
        scratch_shapes=[pltpu.VMEM((width, 3 * part), bf16), pltpu.SemaphoreType.DMA],
        out_shape=[
            jax.ShapeDtypeStruct((rows, width), f32),
            jax.ShapeDtypeStruct((rows, width), bf16),
        ]
        + [jax.ShapeDtypeStruct(p, bf16) for p in pieces],
        cost_estimate=cost(26 * rows * width * part, 40 * width * part),
        compiler_params=pltpu.CompilerParams(vmem_limit_bytes=12 << 20),
        name="qkv_back",
    )(dq, dkv, *x_t, *low_t, *low_t, att, *bases, *blocks)


def bits_of(n):
    bits = n.bit_length() - 1
    if 1 << bits != n:
        raise ValueError("row count")
    return bits


class Links:
    def __init__(self, mesh):
        self.rows = mesh.shape["row"]
        self.cols = mesh.shape["col"]
        self.bits = bits_of(self.rows // 2)

    def locate(self):
        row = lax.axis_index("row")
        col = lax.axis_index("col")
        return row // 2, row % 2, col // (self.cols // 2), col % 2

    def send(self, v, move):
        pairs = []
        for row in range(self.rows):
            for col in range(self.cols):
                ring, x, y, k = move(row // 2, row % 2, col // (self.cols // 2), col % 2)
                pairs.append(
                    (row * self.cols + col, (ring * 2 + x) * self.cols + y * (self.cols // 2) + k)
                )
        return lax.ppermute(v, ("row", "col"), pairs)

    def across(self, v):
        return self.send(v, lambda ring, x, y, k: (ring, x, 1 - y, k))

    def beside(self, v):
        return self.send(v, lambda ring, x, y, k: (ring, x, y, 1 - k))

    def far(self, v):
        return self.send(
            v, lambda ring, x, y, k: (ring, 1 - x, y, k) if k else (ring, x, 1 - y, k)
        )

    def along(self, v):
        return self.send(v, lambda ring, x, y, k: (ring, 1 - x, y, k))

    def turned(self, v, bit):
        return self.send(v, lambda ring, x, y, k: (ring ^ (1 << bit), x, y, k))

    def ring_grow(self, block, bit):
        return jnp.concatenate([block, self.turned(block, bit)], axis=0)

    def ring_gather(self, block, last=0):
        for bit in reversed(range(last, self.bits)):
            block = self.ring_grow(block, bit)
        return block

    def ring_split(self, block):
        own, low = jnp.split(block, 2, axis=0)
        return own, low.astype(bf16)

    def ring_scatter(self, own, low, held=()):
        for bit in range(self.bits):
            if bit > 0:
                own, low = self.ring_split(own)
                low = tie(low, *held)
            own = own + self.turned(low, bit).astype(f32)
        return own


def tie(value, *others):
    return lax.optimization_barrier((value, *others))[0]


class Scatter:
    def __init__(self, links, to_x, to_y, keep):
        self.links, self.keep = links, keep
        by_x = [links.along(v) for v in to_x]
        self.by_x = [by_x[0][0], by_x[0][1]] if len(by_x) == 1 else by_x
        self.by_y = links.across(to_y)

    def second(self):
        to_x = (self.keep[2].astype(f32) + self.by_y[1].astype(f32)).astype(bf16)
        to_y = (self.keep[3].astype(f32) + self.by_x[1].astype(f32)).astype(bf16)
        self.late_x, self.late_y = self.links.along(to_x), self.links.across(to_y)
        return to_x, to_y

    def third(self):
        low = self.keep[0].astype(f32) + self.by_y[0].astype(f32) + self.late_x.astype(f32)
        high = self.keep[1].astype(f32) + self.by_x[0].astype(f32) + self.late_y.astype(f32)
        self.own, self.low = self.links.ring_split(jnp.concatenate([low, high], axis=0))
        return [self.low]

    def last(self, held=()):
        return self.links.ring_scatter(self.own, self.low, held)


def relative_order(links, depth):
    ring, x, _, _ = links.locate()
    where = lax.broadcasted_iota(jnp.int32, (1, links.rows * depth), 1)
    block, inside = where // depth, where % depth
    steps = links.rows // 2
    place = block % steps
    turn = jnp.zeros_like(place)
    for bit in reversed(range(links.bits)):
        turn = turn + (place % 2 << bit)
        place = place // 2
    row = jnp.bitwise_xor(ring, turn) * 2 + jnp.bitwise_xor(x, block // steps)
    return row * depth + inside


def on_device(
    links, tokens, segments, positions, w_qkv, w_out, w_gate_up, w_down, norm_gain, norm_bias, cotangent
):
    ring, x_place, side, core = links.locate()
    depth = w_qkv.shape[0]
    width = tokens.shape[2]
    head_cols = w_qkv.shape[2]
    hid = w_gate_up.shape[2]
    sizes = [hid - hid // 3, hid // 3]
    rows = 2 * tokens.shape[1]
    mine = rows // 2
    part = head_cols + HD

    source = relative_order(links, depth)
    swap = (lax.broadcasted_iota(jnp.int32, (width, width), 0) == source).astype(bf16)

    def split(v):
        high = v.astype(bf16)
        return high, (v - high.astype(f32)).astype(bf16)

    def own_and_other(v):
        own = lax.dynamic_index_in_dim(v, side, 0, keepdims=False)
        return own, lax.dynamic_index_in_dim(v, 1 - side, 0, keepdims=False)

    def from_sequence(own, came):
        first = side == 0
        return jnp.stack([jnp.where(first, own, came), jnp.where(first, came, own)], axis=0)

    out_t = w_out.T
    attn_shard = jnp.concatenate(
        sum(
            [[w_qkv[:, p], out_t[:, p * HD : (p + 1) * HD]] for p in range(3)],
            [],
        ),
        axis=1,
    )
    norms = jnp.concatenate([norm_gain, norm_bias], axis=1)
    norms = jnp.pad(norms, ((0, 0), (0, 128 - norms.shape[1])))
    down_t = w_down.T
    mlp_shards = []
    for h, at in enumerate([0, sizes[0]]):
        cols = slice(at, at + sizes[h])
        pieces = [down_t[:, cols], w_gate_up[:, 0, cols], w_gate_up[:, 1, cols]]
        mlp_shards.append(jnp.concatenate(pieces + ([norms] if h == 0 else []), axis=1))

    small_own, small_other = own_and_other(jnp.stack([segments, positions], axis=1))
    small_came = links.across(small_other)
    tokens_own, tokens_other = own_and_other(tokens)
    tokens_came = links.across(tie(tokens_other, attn_shard, small_other))
    dy_own, dy_other = own_and_other(cotangent)
    dy_came = links.across(tie(dy_other.astype(bf16), attn_shard, small_other))

    odd = core == 1
    ring_a = links.ring_gather(attn_shard)
    x_a, y_a = links.along(ring_a), links.across(ring_a)
    ring_b = links.ring_gather(tie(mlp_shards[0], ring_a))
    turn_a = jnp.where(odd, y_a, x_a)
    attn_w = [ring_a, x_a, y_a, links.far(turn_a)]

    x_abs = jnp.concatenate([tokens_own, tokens_came], axis=0)
    x = dot(x_abs, swap).astype(bf16)
    x_other = links.beside(x)
    small = jnp.concatenate([small_own, small_came], axis=1)
    small = jnp.concatenate([small, links.beside(small)], axis=1)
    qcode, kcode = document_codes(small[0])
    first_quarter, second_quarter = jnp.zeros((1,), jnp.int32), jnp.ones((1,), jnp.int32)
    cosine, sine = rope_tables(small[1])

    ring_b = tie(ring_b, turn_a, cosine, sine, qcode, kcode)
    x_b, y_b = links.along(ring_b), links.across(ring_b)
    ring_c = links.ring_gather(tie(mlp_shards[1], ring_b))
    q, kv, wo = qkv(tie(x, ring_b, dy_came), x_other, cosine, sine, attn_w)
    att_0, logs_0 = attend(first_quarter, q, kv, qcode, kcode)
    att_1, logs_1 = attend(second_quarter, tie(q, att_0), kv, qcode, kcode)
    held_x, held_y = lax.optimization_barrier((x_b, y_b, att_1))[:2]
    turn_b = jnp.where(odd, held_y, held_x)
    mlp_b = [ring_b, x_b, y_b, links.far(turn_b)]
    ring_c = tie(ring_c, turn_b)
    x_c, y_c = links.along(ring_c), links.across(ring_c)
    own, send = project(att_0, tie(att_1, turn_b, ring_c), wo)
    x_t = lax.dot_general(
        swap, tie(x_abs, own), (((0,), (1,)), ((), ())), preferred_element_type=f32
    ).astype(bf16)
    x_t = [x_t, links.beside(x_t)]
    high, low_part = split(tie(dy_own, own))
    dy = jnp.concatenate([dot(high, swap) + dot(low_part, swap), dot(dy_came, swap)], axis=0)
    n1, s1, low, low_t, gains = first_norm(
        x, tie(own, mlp_b[3], x_t[1], dy), links.beside(send), ring_b, x_b
    )
    low_other = links.beside(low)
    act_b_own, feed = mlp(low, None, mlp_b, sizes[0], f32)
    low1_t = [low_t, links.beside(tie(low_t, feed))]
    act_b_other, feed_other = mlp(low_other, None, mlp_b, sizes[0], f32)
    held_x, held_y = lax.optimization_barrier((x_c, y_c, feed))[:2]
    turn_c = jnp.where(odd, held_y, held_x)
    mlp_c = [ring_c, x_c, y_c, links.far(turn_c)]
    act_c_other, send = mlp(tie(low_other, low1_t[1]), feed_other, mlp_c, sizes[1], bf16)
    came = links.beside(send)
    act_c_own, feed = mlp(tie(low, send), feed, mlp_c, sizes[1], f32)
    layer_out, dh2, dfeed, dfeed_t, sums = second_norm(n1, gains, feed, came, dy)
    layer_out = dot(layer_out, swap, NT).astype(bf16)
    layer_came = links.across(layer_out[mine:])
    dfeeds = [dfeed, links.beside(dfeed)]
    dfeeds_t = [dfeed_t, links.beside(dfeed_t)]

    own, other, to_x, to_y, keep = mlp_back(None, dfeeds, dfeeds_t, low1_t, (act_c_own, act_c_other), mlp_c)
    sum_b = Scatter(links, [to_x], to_y, keep)
    own, other, to_x, to_y, keep = mlp_back(
        (tie(own, layer_came), other), dfeeds, dfeeds_t, low1_t, (act_b_own, act_b_other), mlp_b
    )
    came = links.beside(other)
    sum_b.keep = tie(sum_b.keep, own)
    ops_b = sum_b.second()
    sum_c = Scatter(links, [tie(to_x, *ops_b)], tie(to_y, *ops_b), keep)
    dh1, low, low_t = first_back(tie(dh2, *ops_b), own, came, n1, s1, gains, sums)
    lows = [low, links.beside(low)]
    low_t = [low_t, links.beside(low_t)]
    dq, dkv = attend_back(
        second_quarter, q, kv, *lows, wo, att_1, logs_1, qcode, kcode, cosine, sine
    )
    sum_b.keep = tie(sum_b.keep, dq)
    block_b = sum_b.third()
    bases = (dh1, jnp.zeros(low.shape, bf16))
    own, other, to_y, keep_1, to_x_1 = qkv_back(
        bases, tie(dq, *block_b), dkv, x_t, low_t, att_1, attn_w[2:]
    )
    own_b = sum_b.last()
    sum_c.keep = tie(sum_c.keep, own)
    ops_c = sum_c.second()
    dq, dkv = attend_back(
        first_quarter, tie(q, own, *ops_c), kv, *lows, wo, att_0, logs_0, qcode, kcode, cosine, sine
    )
    sum_c.keep = tie(sum_c.keep, dq)
    block_c = sum_c.third()
    own, other, early, middle, to_x_0 = qkv_back(
        (own, other), tie(dq, *block_c, own_b), dkv, x_t, low_t, att_0, attn_w[:2]
    )
    own_c = sum_c.last()
    sum_a = Scatter(links, [to_x_0, to_x_1], to_y, [early[0], middle, early[1], keep_1])
    grad = own + links.beside(other).astype(f32)
    high, low = split(grad)
    grad = dot(high, swap, NT) + dot(low, swap, NT)
    sum_a.keep = tie(sum_a.keep, grad)
    ops_a = sum_a.second()
    own_mlp = [own_c, own_b]
    grad_down = jnp.concatenate([v[:, :n] for v, n in zip(own_mlp, sizes)], axis=1).T
    grad_gate_up = jnp.stack(
        [
            jnp.concatenate([v[:, p * n : (p + 1) * n] for v, n in zip(own_mlp, sizes)], axis=1)
            for p in (1, 2)
        ],
        axis=1,
    )
    block_a = sum_a.third()
    came = links.across(tie(grad[mine:].astype(bf16), *block_a))
    input_grad = from_sequence(grad[:mine], came.astype(f32))
    layer_out = from_sequence(tie(layer_out[:mine], to_x_0), layer_came)
    own_attn = sum_a.last((came, grad_down, grad_gate_up, layer_out))
    thirds = [own_attn[:, p * part : (p + 1) * part] for p in range(3)]
    edge = 3 * part
    return (
        layer_out,
        input_grad,
        jnp.stack([v[:, :head_cols] for v in thirds], axis=1),
        jnp.concatenate([v[:, head_cols:] for v in thirds], axis=1).T,
        grad_gate_up,
        grad_down,
        own_attn[:, edge : edge + 2],
        own_attn[:, edge + 2 : edge + 4],
    )


def solution(mesh):
    in_specs = (
        P(None, ("row", "col"), None),
        P(None, ("row", "col")),
        P(None, ("row", "col")),
        P("row", None, "col"),
        P("col", "row"),
        P("row", None, "col"),
        P("col", "row"),
        P("row", None),
        P("row", None),
        P(None, ("row", "col"), None),
    )
    out_specs = (
        P(None, ("row", "col"), None),
        P(None, ("row", "col"), None),
        P("row", None, "col"),
        P("col", "row"),
        P("row", None, "col"),
        P("col", "row"),
        P("row", None),
        P("row", None),
    )
    return jax.shard_map(
        functools.partial(on_device, Links(mesh)), mesh=mesh, in_specs=in_specs, out_specs=out_specs, check_vma=False
    )
```

profile of v0, /device:TPU:0, one launch (start us, length us, event | category | flops | bytes accessed | tf_op | source)
XLA Modules:
  0.0 277.2 jit_solution(14465070592991320631)
XLA Ops:
  2.6 4.1 %collective-permute-start.1 = (bf16[96,768]{1,0:T(8,128)(2,1)S(1)}, bf16[96,768]{1,0:T(8,128)(2,1)S(1)}, u32[]{:S(2)}, u32[]{:S(2)}) collective-permute-start(bf16[96,768]{1,0:T(8,128)(2,1)S(1)} %concatenate.58), channel_id=1, source_target_pairs={{0,16},{1,17},{2,18},{3,19},{4,20},{5,21},{6,22},{7,23},{8,24},{9,... | collective-permute-start | bytes 442376 | tf_op jit(solution)/shard_map/ppermute | solution.py:716
  7.6 1.6 collective-permute-start.7
  9.2 2.3 dynamic-slice_bitcast_fusion.2
  12.0 1.5 collective-permute-start.9
  14.5 1.6 collective-permute-start.2
  16.2 7.8 %collective-permute-done.2 = bf16[192,768]{1,0:T(8,128)(2,1)S(1)} collective-permute-done((bf16[192,768]{1,0:T(8,128)(2,1)S(1)}, bf16[192,768]{1,0:T(8,128)(2,1)S(1)}, u32[]{:S(2)}, u32[]{:S(2)}) %collective-permute-start.2) | collective-permute-done | bytes 294944 | tf_op jit(solution)/shard_map/ppermute | solution.py:716
  25.5 1.9 fusion.35
  27.4 1.6 collective-permute-start.5
  29.0 1.5 collective-permute-start.6
  30.5 10.5 %collective-permute-done.3 = bf16[96,1664]{1,0:T(8,128)(2,1)S(1)} collective-permute-done((bf16[96,1664]{1,0:T(8,128)(2,1)S(1)}, bf16[96,1664]{1,0:T(8,128)(2,1)S(1)}, u32[]{:S(2)}, u32[]{:S(2)}) %collective-permute-start.3) | collective-permute-done | bytes 319520 | tf_op jit(solution)/shard_map/ppermute | solution.py:716
  43.8 12.6 %collective-permute-done.4 = bf16[192,1664]{1,0:T(8,128)(2,1)S(1)} collective-permute-done((bf16[192,1664]{1,0:T(8,128)(2,1)S(1)}, bf16[192,1664]{1,0:T(8,128)(2,1)S(1)}, u32[]{:S(2)}, u32[]{:S(2)}) %collective-permute-start.4) | collective-permute-done | bytes 639008 | tf_op jit(solution)/shard_map/ppermute | solution.py:716
  56.5 1.7 collective-permute-start.14
  58.3 1.6 collective-permute-start.12
  59.8 1.5 collective-permute-start.13
  61.3 3.4 %collective-permute-done.14 = bf16[96,768]{1,0:T(8,128)(2,1)S(1)} collective-permute-done((bf16[96,768]{1,0:T(8,128)(2,1)S(1)}, bf16[96,768]{1,0:T(8,128)(2,1)S(1)}, u32[]{:S(2)}, u32[]{:S(2)}) %collective-permute-start.14) | collective-permute-done | bytes 147488 | tf_op jit(solution)/shard_map/ppermute | solution.py:716
  65.6 5.3 %qkv.1 = (bf16[1024,512]{1,0:T(8,128)(2,1)S(1)}, bf16[1024,1024]{1,0:T(8,128)(2,1)S(1)}, bf16[768,512]{1,0:T(8,128)(2,1)S(1)}) custom-call(bf16[512,768]{1,0:T(8,128)(2,1)S(1)} %fusion.9.own_ref.x_ref, bf16[512,768]{1,0:T(8,128)(2,1)S(1)} %collective-permute-done.10.other_ref, f32[1024,128]{1,0:T(8,128)S(1)} %get-tuple-element.247.cos_ref, ...), custom_call_target="tpu_custom_call" | custom-call | flops 2415919104 | bytes 7864320 | tf_op jit(solution)/shard_map/qkv/pallas_call | solution.py:131
  70.9 7.6 %attend.2 = (bf16[1024,256]{1,0:T(8,128)(2,1)S(1)}, f32[8,1024]{1,0:T(8,128)S(1)}) custom-call(s32[1]{0:T(128)} %constant.169.clone.1.quarter_ref, bf16[1024,512]{1,0:T(8,128)(2,1)S(1)} %get-tuple-element.168.q_ref, bf16[1024,1024]{1,0:T(8,128)(2,1)S(1)} %get-tuple-element.105.kv_ref, bf16[1024,128]{1,0:T(8,128)(2,1)S(1)} %fusion.37.qcode_ref, ...), custom_call_target="tpu_custom_call" | custom-call | flops 4294967296 | bytes 3145728 | tf_op jit(solution)/shard_map/attend/pallas_call | solution.py:222
  78.5 7.6 %attend.3 = (bf16[1024,256]{1,0:T(8,128)(2,1)S(1)}, f32[8,1024]{1,0:T(8,128)S(1)}) custom-call(s32[1]{0:T(128)} %constant.182.clone.1.quarter_ref, bf16[1024,512]{1,0:T(8,128)(2,1)S(1)} %get-tuple-element.168.q_ref, bf16[1024,1024]{1,0:T(8,128)(2,1)S(1)} %get-tuple-element.105.kv_ref, bf16[1024,128]{1,0:T(8,128)(2,1)S(1)} %fusion.37.qcode_ref, ...), custom_call_target="tpu_custom_call" | custom-call | flops 4294967296 | bytes 3145728 | tf_op jit(solution)/shard_map/attend/pallas_call | solution.py:222
  88.8 1.6 collective-permute-start.16
  96.2 16.3 %collective-permute-done.16.rest_3_.rest_13_ = bf16[384,1664]{1,0:T(8,128)(2,1)S(1)} collective-permute-done((bf16[384,1664]{1,0:T(8,128)(2,1)S(1)}, bf16[384,1664]{1,0:T(8,128)(2,1)S(1)}, u32[]{:S(2)}, u32[]{:S(2)}) %collective-permute-start.16) | collective-permute-done | bytes 1277984 | tf_op jit(solution)/shard_map/ppermute | solution.py:716
  113.5 4.8 %mlp.4 = (bf16[2,3,512,512]{3,2,1,0:T(8,128)(2,1)S(1)}, f32[512,768]{1,0:T(8,128)S(1)}) custom-call(bf16[512,768]{1,0:T(8,128)(2,1)S(1)} %get-tuple-element.131.low_ref, bf16[384,1664]{1,0:T(8,128)(2,1)S(1)} %pad_maximum_fusion.2.norm_a_ref.rest_0_.rest_10_, bf16[384,1664]{1,0:T(8,128)(2,1)S(1)} %collective-permute-done.12.norm_b_ref.rest_1_.rest_11_, ...), custom_call_target="tpu_custom_call" | custom-call | flops 2415919104 | bytes 11796480 | tf_op jit(solution)/shard_map/mlp/pallas_call | solution.py:434
  119.0 1.6 collective-permute-start.23
  120.8 4.9 %mlp.5 = (bf16[2,3,512,512]{3,2,1,0:T(8,128)(2,1)S(1)}, f32[512,768]{1,0:T(8,128)S(1)}) custom-call(bf16[512,768]{1,0:T(8,128)(2,1)S(1)} %collective-permute-done.19.low_ref, bf16[384,1664]{1,0:T(8,128)(2,1)S(1)} %pad_maximum_fusion.2.norm_a_ref.rest_0_.rest_10_, bf16[384,1664]{1,0:T(8,128)(2,1)S(1)} %collective-permute-done.12.norm_b_ref.rest_1_.rest_11_, ...), custom_call_target="tpu_custom_call" | custom-call | flops 2415919104 | bytes 11796480 | tf_op jit(solution)/shard_map/mlp/pallas_call | solution.py:434
  125.7 3.2 %collective-permute-done.23.rest_4_.rest_11_ = bf16[384,768]{1,0:T(8,128)(2,1)S(1)} collective-permute-done((bf16[384,768]{1,0:T(8,128)(2,1)S(1)}, bf16[384,768]{1,0:T(8,128)(2,1)S(1)}, u32[]{:S(2)}, u32[]{:S(2)}) %collective-permute-start.23) | collective-permute-done | bytes 589856 | tf_op jit(solution)/shard_map/ppermute | solution.py:716
  128.9 2.5 mlp.6
  131.5 2.5 mlp.7
  134.0 1.7 second_norm.1
  138.0 1.5 collective-permute-start.27
  139.5 8.0 %mlp_back.2 = (f32[512,768]{1,0:T(8,128)S(1)}, f32[512,768]{1,0:T(8,128)S(1)}, bf16[2,192,768]{2,1,0:T(8,128)(2,1)S(1)}, bf16[2,192,768]{2,1,0:T(8,128)(2,1)S(1)}, bf16[4,192,768]{2,1,0:T(8,128)(2,1)S(1)}) custom-call(bf16[512,768]{1,0:T(8,128)(2,1)S(1)} %get-tuple-element.135.rest_0_, bf16[512,768]{1,0:T(8,128)(2,1)S(1)} %collective-permute-done.25.rest_1_, ...), custom_call_target="tpu_custom_call" | custom-call | flops 4831838208 | bytes 19660800 | tf_op jit(solution)/shard_map/mlp_back/pallas_call | solution.py:556
  149.4 1.5 collective-permute-start.28
  151.0 13.8 %mlp_back.3 = (f32[512,768]{1,0:T(8,128)S(1)}, bf16[512,768]{1,0:T(8,128)(2,1)S(1)}, bf16[2,192,1536]{2,1,0:T(8,128)(2,1)S(1)}, bf16[2,192,1536]{2,1,0:T(8,128)(2,1)S(1)}, bf16[4,192,1536]{2,1,0:T(8,128)(2,1)S(1)}) custom-call(bf16[512,768]{1,0:T(8,128)(2,1)S(1)} %get-tuple-element.135.rest_0_, bf16[512,768]{1,0:T(8,128)(2,1)S(1)} %collective-permute-done.25.rest_1_, ...), custom_call_target="tpu_custom_call" | custom-call | flops 9663676416 | bytes 39321600 | tf_op jit(solution)/shard_map/mlp_back/pallas_call | solution.py:556
  167.1 2.0 first_back.1
  179.7 1.6 copy-done.29
  182.5 14.5 %attend_back.2 = (bf16[1024,256]{1,0:T(8,128)(2,1)S(1)}, bf16[1024,512]{1,0:T(8,128)(2,1)S(1)}) custom-call(s32[1]{0:T(128)} %constant.182.clone.1.quarter_ref, bf16[1024,512]{1,0:T(8,128)(2,1)S(1)} %copy-done.32, bf16[1024,1024]{1,0:T(8,128)(2,1)S(1)} %copy-done.29, bf16[512,768]{1,0:T(8,128)(2,1)} %get-tuple-element.153.own_ref, ...), custom_call_target="tpu_custom_call" | custom-call | flops 10737418240 | bytes 7864320 | tf_op jit(solution)/shard_map/attend_back/pallas_call | solution.py:326
  197.2 1.5 collective-permute-start.38
  198.8 4.1 %qkv_back.2 = (f32[512,768]{1,0:T(8,128)S(1)}, bf16[512,768]{1,0:T(8,128)(2,1)S(1)}, bf16[2,192,896]{2,1,0:T(8,128)(2,1)S(1)}, bf16[192,896]{1,0:T(8,128)(2,1)S(1)}, bf16[192,896]{1,0:T(8,128)(2,1)S(1)}) custom-call(bf16[1024,256]{1,0:T(8,128)(2,1)S(1)} %get-tuple-element.157.dq_ref, bf16[1024,512]{1,0:T(8,128)(2,1)S(1)} %get-tuple-element.158.dkv_ref, ...), custom_call_target="tpu_custom_call" | custom-call | flops 2617245696 | bytes 7864320 | tf_op jit(solution)/shard_map/qkv_back/pallas_call | solution.py:670
  202.9 2.8 collective-permute-done.35
  208.1 1.9 collective-permute-start.39
  210.1 14.4 %attend_back.3 = (bf16[1024,256]{1,0:T(8,128)(2,1)S(1)}, bf16[1024,512]{1,0:T(8,128)(2,1)S(1)}) custom-call(s32[1]{0:T(128)} %constant.169.clone.1.quarter_ref, bf16[1024,512]{1,0:T(8,128)(2,1)S(1)} %copy-done.33, bf16[1024,1024]{1,0:T(8,128)(2,1)S(1)} %copy-done.30, bf16[512,768]{1,0:T(8,128)(2,1)} %get-tuple-element.153.own_ref, ...), custom_call_target="tpu_custom_call" | custom-call | flops 10737418240 | bytes 7864320 | tf_op jit(solution)/shard_map/attend_back/pallas_call | solution.py:326
  227.0 3.8 %qkv_back.3 = (f32[512,768]{1,0:T(8,128)S(1)}, bf16[512,768]{1,0:T(8,128)(2,1)S(1)}, bf16[2,192,896]{2,1,0:T(8,128)(2,1)S(1)}, bf16[192,896]{1,0:T(8,128)(2,1)S(1)}, bf16[192,896]{1,0:T(8,128)(2,1)S(1)}) custom-call(bf16[1024,256]{1,0:T(8,128)(2,1)S(1)} %get-tuple-element.172.dq_ref, bf16[1024,512]{1,0:T(8,128)(2,1)S(1)} %get-tuple-element.173.dkv_ref, ...), custom_call_target="tpu_custom_call" | custom-call | flops 2617245696 | bytes 7864320 | tf_op jit(solution)/shard_map/qkv_back/pallas_call | solution.py:670
  232.0 1.5 collective-permute-start.41
  233.5 5.7 %collective-permute-done.49 = bf16[192,1536]{1,0:T(8,128)(2,1)S(1)} collective-permute-done((bf16[192,1536]{1,0:T(8,128)(2,1)S(1)}, bf16[192,1536]{1,0:T(8,128)(2,1)S(1)}, u32[]{:S(2)}, u32[]{:S(2)}) %collective-permute-start.49) | collective-permute-done | bytes 589856 | tf_op jit(solution)/shard_map/ppermute | solution.py:716
  239.6 2.3 collective-permute-start.50
  245.7 7.0 %collective-permute-done.50 = bf16[96,1536]{1,0:T(8,128)(2,1)S(1)} collective-permute-done((bf16[96,1536]{1,0:T(8,128)(2,1)S(1)}, bf16[96,1536]{1,0:T(8,128)(2,1)S(1)}, u32[]{:S(2)}, u32[]{:S(2)}) %collective-permute-start.50) | collective-permute-done | bytes 294944 | tf_op jit(solution)/shard_map/ppermute | solution.py:716
  256.5 5.7 %collective-permute-done.47 = bf16[192,896]{1,0:T(8,128)(2,1)S(1)} collective-permute-done((bf16[192,896]{1,0:T(8,128)(2,1)S(1)}, bf16[192,896]{1,0:T(8,128)(2,1)S(1)}, u32[]{:S(2)}, u32[]{:S(2)}) %collective-permute-start.47) | collective-permute-done | bytes 344096 | tf_op jit(solution)/shard_map/ppermute | solution.py:716
  262.3 2.2 collective-permute-done.44
  264.6 3.1 %collective-permute-start.51 = (bf16[96,896]{1,0:T(8,128)(2,1)S(1)}, bf16[96,896]{1,0:T(8,128)(2,1)S(1)}, u32[]{:S(2)}, u32[]{:S(2)}) collective-permute-start(bf16[96,896]{1,0:T(8,128)(2,1)S(1)} %split.40), channel_id=1, source_target_pairs={{0,16},{1,17},{2,18},{3,19},{4,20},{5,21},{6,22},{7,23},{8,24},{9,... | collective-permute-start | bytes 516104 | tf_op jit(solution)/shard_map/ppermute | solution.py:716
  269.1 4.8 %collective-permute-done.51 = bf16[96,896]{1,0:T(8,128)(2,1)S(1)} collective-permute-done((bf16[96,896]{1,0:T(8,128)(2,1)S(1)}, bf16[96,896]{1,0:T(8,128)(2,1)S(1)}, u32[]{:S(2)}, u32[]{:S(2)}) %collective-permute-start.51) | collective-permute-done | bytes 172064 | tf_op jit(solution)/shard_map/ppermute | solution.py:716
  (256 shorter events, 56.6 us)
Async XLA Ops:
  2.6 11.9 %collective-permute-start.1 = (bf16[96,768]{1,0:T(8,128)(2,1)S(1)}, bf16[96,768]{1,0:T(8,128)(2,1)S(1)}, u32[]{:S(2)}, u32[]{:S(2)}) collective-permute-start(bf16[96,768]{1,0:T(8,128)(2,1)S(1)} %concatenate.58), channel_id=1, source_target_pairs={{0,16},{1,17},{2,18},{3,19},{4,20},{5,21},{6,22},{7,23},{8,24},{9,... | collective-permute-start | bytes 442376 | tf_op jit(solution)/shard_map/ppermute | solution.py:716
  7.6 6.8 %collective-permute-start.7 = (s32[2,256]{1,0:T(2,128)S(1)}, s32[2,256]{1,0:T(2,128)S(1)}, u32[]{:S(2)}, u32[]{:S(2)}) collective-permute-start(s32[2,256]{1,0:T(2,128)S(1)} %bitcast.105), channel_id=1, source_target_pairs={{0,2},{1,3},{2,0},{3,1},{4,6},{5,7},{6,4},{7,5},{8,10},{9,11},{10,... | collective-permute-start | bytes 6152 | tf_op jit(solution)/shard_map/ppermute | solution.py:716
  11.5 29.9 %collective-permute-start = (bf16[256,768]{1,0:T(8,128)(2,1)}, bf16[256,768]{1,0:T(8,128)(2,1)S(1)}, u32[]{:S(2)}, u32[]{:S(2)}) collective-permute-start(bf16[256,768]{1,0:T(8,128)(2,1)} %get-tuple-element.99), channel_id=1, source_target_pairs={{0,2},{1,3},{2,0},{3,1},{4,6},{5,7},{6,4},{7,5},{8,10},{9,11},{10,... | collective-permute-start | bytes 1179656 | tf_op jit(solution)/shard_map/ppermute | solution.py:716
  12.0 47.8 %collective-permute-start.9 = (bf16[256,768]{1,0:T(8,128)(2,1)}, bf16[256,768]{1,0:T(8,128)(2,1)S(1)}, u32[]{:S(2)}, u32[]{:S(2)}) collective-permute-start(bf16[256,768]{1,0:T(8,128)(2,1)} %get-tuple-element.102), channel_id=1, source_target_pairs={{0,2},{1,3},{2,0},{3,1},{4,6},{5,7},{6,4},{7,5},{8,10},{9,11},{10,... | collective-permute-start | bytes 1179656 | tf_op jit(solution)/shard_map/ppermute | solution.py:716
  14.5 9.5 %collective-permute-start.2 = (bf16[192,768]{1,0:T(8,128)(2,1)S(1)}, bf16[192,768]{1,0:T(8,128)(2,1)S(1)}, u32[]{:S(2)}, u32[]{:S(2)}) collective-permute-start(bf16[192,768]{1,0:T(8,128)(2,1)S(1)} %pad_maximum_fusion.9), channel_id=1, source_target_pairs={{0,8},{1,9},{2,10},{3,11},{4,12},{5,13},{6,14},{7,15},{8,0},{9,1},... | collective-permute-start | bytes 884744 | tf_op jit(solution)/shard_map/ppermute | solution.py:716
  24.0 17.0 %collective-permute-start.3 = (bf16[96,1664]{1,0:T(8,128)(2,1)S(1)}, bf16[96,1664]{1,0:T(8,128)(2,1)S(1)}, u32[]{:S(2)}, u32[]{:S(2)}) collective-permute-start(bf16[96,1664]{1,0:T(8,128)(2,1)S(1)} %fusion.43), channel_id=1, source_target_pairs={{0,16},{1,17},{2,18},{3,19},{4,20},{5,21},{6,22},{7,23},{8,24},{9,... | collective-permute-start | bytes 958472 | tf_op jit(solution)/shard_map/ppermute | solution.py:716
  27.4 15.7 %collective-permute-start.5 = (bf16[384,768]{1,0:T(8,128)(2,1)S(1)}, bf16[384,768]{1,0:T(8,128)(2,1)S(1)}, u32[]{:S(2)}, u32[]{:S(2)}) collective-permute-start(bf16[384,768]{1,0:T(8,128)(2,1)S(1)} %pad_maximum_fusion.6.rest_0_.top_ref), channel_id=1, source_target_pairs={{0,2},{1,3},{2,0},{3,1},{4,6},{5,7},{6,4},{7,5},{8,10},{9,11},{10,... | collective-permute-start | bytes 1769480 | tf_op jit(solution)/shard_map/ppermute | solution.py:716
  29.0 14.2 %collective-permute-start.6 = (bf16[384,768]{1,0:T(8,128)(2,1)S(1)}, bf16[384,768]{1,0:T(8,128)(2,1)S(1)}, u32[]{:S(2)}, u32[]{:S(2)}) collective-permute-start(bf16[384,768]{1,0:T(8,128)(2,1)S(1)} %pad_maximum_fusion.6.rest_0_.top_ref), channel_id=1, source_target_pairs={{0,4},{1,5},{2,6},{3,7},{4,0},{5,1},{6,2},{7,3},{8,12},{9,13},{10,... | collective-permute-start | bytes 1769480 | tf_op jit(solution)/shard_map/ppermute | solution.py:716
  41.0 15.3 %collective-permute-start.4 = (bf16[192,1664]{1,0:T(8,128)(2,1)S(1)}, bf16[192,1664]{1,0:T(8,128)(2,1)S(1)}, u32[]{:S(2)}, u32[]{:S(2)}) collective-permute-start(bf16[192,1664]{1,0:T(8,128)(2,1)S(1)} %pad_maximum_fusion.5), channel_id=1, source_target_pairs={{0,8},{1,9},{2,10},{3,11},{4,12},{5,13},{6,14},{7,15},{8,0},{9,1},... | collective-permute-start | bytes 1916936 | tf_op jit(solution)/shard_map/ppermute | solution.py:716
  42.2 23.3 %collective-permute-start.10 = (bf16[512,768]{1,0:T(8,128)(2,1)S(1)}, bf16[512,768]{1,0:T(8,128)(2,1)S(1)}, u32[]{:S(2)}, u32[]{:S(2)}) collective-permute-start(bf16[512,768]{1,0:T(8,128)(2,1)S(1)} %fusion.9.own_ref.x_ref), channel_id=1, source_target_pairs={{0,1},{1,0},{2,3},{3,2},{4,5},{5,4},{6,7},{7,6},{8,9},{9,8},{10,11... | collective-permute-start | bytes 2359304 | tf_op jit(solution)/shard_map/ppermute | solution.py:716
  43.2 22.3 %collective-permute-start.11 = (bf16[384,768]{1,0:T(8,128)(2,1)S(1)}, bf16[384,768]{1,0:T(8,128)(2,1)S(1)}, u32[]{:S(2)}, u32[]{:S(2)}) collective-permute-start(bf16[384,768]{1,0:T(8,128)(2,1)S(1)} %broadcast_select_fusion.2), channel_id=1, source_target_pairs={{0,2},{1,5},{2,0},{3,7},{4,6},{5,1},{6,4},{7,3},{8,10},{9,13},{10,... | collective-permute-start | bytes 1769480 | tf_op jit(solution)/shard_map/ppermute | solution.py:716
  56.5 8.3 %collective-permute-start.14 = (bf16[96,768]{1,0:T(8,128)(2,1)S(1)}, bf16[96,768]{1,0:T(8,128)(2,1)S(1)}, u32[]{:S(2)}, u32[]{:S(2)}) collective-permute-start(bf16[96,768]{1,0:T(8,128)(2,1)S(1)} %pad_maximum_fusion.12), channel_id=1, source_target_pairs={{0,16},{1,17},{2,18},{3,19},{4,20},{5,21},{6,22},{7,23},{8,24},{9,... | collective-permute-start | bytes 442376 | tf_op jit(solution)/shard_map/ppermute | solution.py:716
  58.3 29.2 %collective-permute-start.12 = (bf16[384,1664]{1,0:T(8,128)(2,1)S(1)}, bf16[384,1664]{1,0:T(8,128)(2,1)S(1)}, u32[]{:S(2)}, u32[]{:S(2)}) collective-permute-start(bf16[384,1664]{1,0:T(8,128)(2,1)S(1)} %pad_maximum_fusion.2.norm_a_ref.rest_0_.rest_10_), channel_id=1, source_target_pairs={{0,4},{1,5},{2,6},{3,7},{4,0},{5,1},{6,2},{7,3},{8,12},{9,13},{10,... | collective-permute-start | bytes 3833864 | tf_op jit(solution)/shard_map/ppermute | solution.py:716
  59.8 28.9 %collective-permute-start.13 = (bf16[384,1664]{1,0:T(8,128)(2,1)S(1)}, bf16[384,1664]{1,0:T(8,128)(2,1)S(1)}, u32[]{:S(2)}, u32[]{:S(2)}) collective-permute-start(bf16[384,1664]{1,0:T(8,128)(2,1)S(1)} %pad_maximum_fusion.2.norm_a_ref.rest_0_.rest_10_), channel_id=1, source_target_pairs={{0,2},{1,3},{2,0},{3,1},{4,6},{5,7},{6,4},{7,5},{8,10},{9,11},{10,... | collective-permute-start | bytes 3833864 | tf_op jit(solution)/shard_map/ppermute | solution.py:716
  64.8 21.4 %collective-permute-start.15 = (bf16[192,768]{1,0:T(8,128)(2,1)S(1)}, bf16[192,768]{1,0:T(8,128)(2,1)S(1)}, u32[]{:S(2)}, u32[]{:S(2)}) collective-permute-start(bf16[192,768]{1,0:T(8,128)(2,1)S(1)} %pad_maximum_fusion.10), channel_id=1, source_target_pairs={{0,8},{1,9},{2,10},{3,11},{4,12},{5,13},{6,14},{7,15},{8,0},{9,1},... | collective-permute-start | bytes 884744 | tf_op jit(solution)/shard_map/ppermute | solution.py:716
  88.8 23.6 %collective-permute-start.16 = (bf16[384,1664]{1,0:T(8,128)(2,1)S(1)}, bf16[384,1664]{1,0:T(8,128)(2,1)S(1)}, u32[]{:S(2)}, u32[]{:S(2)}) collective-permute-start(bf16[384,1664]{1,0:T(8,128)(2,1)S(1)} %broadcast_select_fusion), channel_id=1, source_target_pairs={{0,2},{1,5},{2,0},{3,7},{4,6},{5,1},{6,4},{7,3},{8,10},{9,13},{10,... | collective-permute-start | bytes 3833864 | tf_op jit(solution)/shard_map/ppermute | solution.py:716
  92.3 3.9 %collective-permute-start.17 = (bf16[768,512]{1,0:T(8,128)(2,1)S(1)}, bf16[768,512]{1,0:T(8,128)(2,1)S(1)}, u32[]{:S(2)}, u32[]{:S(2)}) collective-permute-start(bf16[768,512]{1,0:T(8,128)(2,1)S(1)} %convolution_convert_fusion.x_a_ref), channel_id=1, source_target_pairs={{0,1},{1,0},{2,3},{3,2},{4,5},{5,4},{6,7},{7,6},{8,9},{9,8},{10,11... | collective-permute-start | bytes 2359304 | tf_op jit(solution)/shard_map/ppermute | solution.py:716
  92.4 20.1 %collective-permute-start.18 = (bf16[512,768]{1,0:T(8,128)(2,1)S(1)}, bf16[512,768]{1,0:T(8,128)(2,1)S(1)}, u32[]{:S(2)}, u32[]{:S(2)}) collective-permute-start(bf16[512,768]{1,0:T(8,128)(2,1)S(1)} %get-tuple-element.119), channel_id=1, source_target_pairs={{0,1},{1,0},{2,3},{3,2},{4,5},{5,4},{6,7},{7,6},{8,9},{9,8},{10,11... | collective-permute-start | bytes 2359304 | tf_op jit(solution)/shard_map/ppermute | solution.py:716
  93.5 25.3 %collective-permute-start.21 = (bf16[384,768]{1,0:T(8,128)(2,1)S(1)}, bf16[384,768]{1,0:T(8,128)(2,1)S(1)}, u32[]{:S(2)}, u32[]{:S(2)}) collective-permute-start(bf16[384,768]{1,0:T(8,128)(2,1)S(1)} %pad_maximum_fusion.7.rest_1_.rest_8_), channel_id=1, source_target_pairs={{0,4},{1,5},{2,6},{3,7},{4,0},{5,1},{6,2},{7,3},{8,12},{9,13},{10,... | collective-permute-start | bytes 1769480 | tf_op jit(solution)/shard_map/ppermute | solution.py:716
  94.2 24.7 %collective-permute-start.22 = (bf16[384,768]{1,0:T(8,128)(2,1)S(1)}, bf16[384,768]{1,0:T(8,128)(2,1)S(1)}, u32[]{:S(2)}, u32[]{:S(2)}) collective-permute-start(bf16[384,768]{1,0:T(8,128)(2,1)S(1)} %pad_maximum_fusion.7.rest_1_.rest_8_), channel_id=1, source_target_pairs={{0,2},{1,3},{2,0},{3,1},{4,6},{5,7},{6,4},{7,5},{8,10},{9,11},{10,... | collective-permute-start | bytes 1769480 | tf_op jit(solution)/shard_map/ppermute | solution.py:716
  113.4 7.1 %collective-permute-start.19 = (bf16[512,768]{1,0:T(8,128)(2,1)S(1)}, bf16[512,768]{1,0:T(8,128)(2,1)S(1)}, u32[]{:S(2)}, u32[]{:S(2)}) collective-permute-start(bf16[512,768]{1,0:T(8,128)(2,1)S(1)} %get-tuple-element.131.low_ref), channel_id=1, source_target_pairs={{0,1},{1,0},{2,3},{3,2},{4,5},{5,4},{6,7},{7,6},{8,9},{9,8},{10,11... | collective-permute-start | bytes 2359304 | tf_op jit(solution)/shard_map/ppermute | solution.py:716
  119.0 9.9 %collective-permute-start.23 = (bf16[384,768]{1,0:T(8,128)(2,1)S(1)}, bf16[384,768]{1,0:T(8,128)(2,1)S(1)}, u32[]{:S(2)}, u32[]{:S(2)}) collective-permute-start(bf16[384,768]{1,0:T(8,128)(2,1)S(1)} %broadcast_select_fusion.1), channel_id=1, source_target_pairs={{0,2},{1,5},{2,0},{3,7},{4,6},{5,1},{6,4},{7,3},{8,10},{9,13},{10,... | collective-permute-start | bytes 1769480 | tf_op jit(solution)/shard_map/ppermute | solution.py:716
  135.7 3.8 %collective-permute-start.25 = (bf16[512,768]{1,0:T(8,128)(2,1)S(1)}, bf16[512,768]{1,0:T(8,128)(2,1)S(1)}, u32[]{:S(2)}, u32[]{:S(2)}) collective-permute-start(bf16[512,768]{1,0:T(8,128)(2,1)S(1)} %get-tuple-element.135.rest_0_), channel_id=1, source_target_pairs={{0,1},{1,0},{2,3},{3,2},{4,5},{5,4},{6,7},{7,6},{8,9},{9,8},{10,11... | collective-permute-start | bytes 2359304 | tf_op jit(solution)/shard_map/ppermute | solution.py:716
  136.2 3.3 %collective-permute-start.26 = (bf16[768,512]{1,0:T(8,128)(2,1)S(1)}, bf16[768,512]{1,0:T(8,128)(2,1)S(1)}, u32[]{:S(2)}, u32[]{:S(2)}) collective-permute-start(bf16[768,512]{1,0:T(8,128)(2,1)S(1)} %get-tuple-element.136.rest_2_), channel_id=1, source_target_pairs={{0,1},{1,0},{2,3},{3,2},{4,5},{5,4},{6,7},{7,6},{8,9},{9,8},{10,11... | collective-permute-start | bytes 2359304 | tf_op jit(solution)/shard_map/ppermute | solution.py:716
  138.0 11.5 %collective-permute-start.27 = (bf16[256,768]{1,0:T(8,128)(2,1)S(1)}, bf16[256,768]{1,0:T(8,128)(2,1)S(1)}, u32[]{:S(2)}, u32[]{:S(2)}) collective-permute-start(bf16[256,768]{1,0:T(8,128)(2,1)S(1)} %get-tuple-element.215), channel_id=1, source_target_pairs={{0,2},{1,3},{2,0},{3,1},{4,6},{5,7},{6,4},{7,5},{8,10},{9,11},{10,... | collective-permute-start | bytes 1179656 | tf_op jit(solution)/shard_map/ppermute | solution.py:716
  147.5 17.3 %collective-permute-start.29 = (bf16[2,192,768]{2,1,0:T(8,128)(2,1)S(1)}, bf16[2,192,768]{2,1,0:T(8,128)(2,1)S(1)}, u32[]{:S(2)}, u32[]{:S(2)}) collective-permute-start(bf16[2,192,768]{2,1,0:T(8,128)(2,1)S(1)} %get-tuple-element.148), channel_id=1, source_target_pairs={{0,4},{1,5},{2,6},{3,7},{4,0},{5,1},{6,2},{7,3},{8,12},{9,13},{10,... | collective-permute-start | bytes 1769480 | tf_op jit(solution)/shard_map/ppermute | solution.py:716
  149.4 15.4 %collective-permute-start.28 = (bf16[2,192,768]{2,1,0:T(8,128)(2,1)S(1)}, bf16[2,192,768]{2,1,0:T(8,128)(2,1)S(1)}, u32[]{:S(2)}, u32[]{:S(2)}) collective-permute-start(bf16[2,192,768]{2,1,0:T(8,128)(2,1)S(1)} %get-tuple-element.147), channel_id=1, source_target_pairs={{0,2},{1,3},{2,0},{3,1},{4,6},{5,7},{6,4},{7,5},{8,10},{9,11},{10,... | collective-permute-start | bytes 1769480 | tf_op jit(solution)/shard_map/ppermute | solution.py:716
  170.3 4.2 %collective-permute-start.31 = (bf16[512,768]{1,0:T(8,128)(2,1)}, bf16[512,768]{1,0:T(8,128)(2,1)}, u32[]{:S(2)}, u32[]{:S(2)}) collective-permute-start(bf16[512,768]{1,0:T(8,128)(2,1)} %get-tuple-element.153.own_ref), channel_id=1, source_target_pairs={{0,1},{1,0},{2,3},{3,2},{4,5},{5,4},{6,7},{7,6},{8,9},{9,8},{10,11... | collective-permute-start | bytes 2359304 | tf_op jit(solution)/shard_map/ppermute | solution.py:716
  170.4 26.6 %collective-permute-start.32 = (bf16[192,768]{1,0:T(8,128)(2,1)}, bf16[192,768]{1,0:T(8,128)(2,1)S(1)}, u32[]{:S(2)}, u32[]{:S(2)}) collective-permute-start(bf16[192,768]{1,0:T(8,128)(2,1)} %get-tuple-element.210), channel_id=1, source_target_pairs={{0,2},{1,3},{2,0},{3,1},{4,6},{5,7},{6,4},{7,5},{8,10},{9,11},{10,... | collective-permute-start | bytes 884744 | tf_op jit(solution)/shard_map/ppermute | solution.py:716
  171.2 36.7 %collective-permute-start.37 = (bf16[192,768]{1,0:T(8,128)(2,1)}, bf16[192,768]{1,0:T(8,128)(2,1)S(1)}, u32[]{:S(2)}, u32[]{:S(2)}) collective-permute-start(bf16[192,768]{1,0:T(8,128)(2,1)} %get-tuple-element.211), channel_id=1, source_target_pairs={{0,4},{1,5},{2,6},{3,7},{4,0},{5,1},{6,2},{7,3},{8,12},{9,13},{10,... | collective-permute-start | bytes 884744 | tf_op jit(solution)/shard_map/ppermute | solution.py:716
  171.7 33.9 %collective-permute-start.35 = (bf16[2,192,1536]{2,1,0:T(8,128)(2,1)}, bf16[2,192,1536]{2,1,0:T(8,128)(2,1)S(1)}, u32[]{:S(2)}, u32[]{:S(2)}) collective-permute-start(bf16[2,192,1536]{2,1,0:T(8,128)(2,1)} %copy-done.24), channel_id=1, source_target_pairs={{0,4},{1,5},{2,6},{3,7},{4,0},{5,1},{6,2},{7,3},{8,12},{9,13},{10,... | collective-permute-start | bytes 3538952 | tf_op jit(solution)/shard_map/ppermute | solution.py:716
  173.2 32.5 %collective-permute-start.34 = (bf16[2,192,1536]{2,1,0:T(8,128)(2,1)}, bf16[2,192,1536]{2,1,0:T(8,128)(2,1)S(1)}, u32[]{:S(2)}, u32[]{:S(2)}) collective-permute-start(bf16[2,192,1536]{2,1,0:T(8,128)(2,1)} %copy-done.23), channel_id=1, source_target_pairs={{0,2},{1,3},{2,0},{3,1},{4,6},{5,7},{6,4},{7,5},{8,10},{9,11},{10,... | collective-permute-start | bytes 3538952 | tf_op jit(solution)/shard_map/ppermute | solution.py:716
  174.5 24.2 %collective-permute-start.33 = (bf16[768,640]{1,0:T(8,128)(2,1)S(1)}, bf16[768,640]{1,0:T(8,128)(2,1)S(1)}, u32[]{:S(2)}, u32[]{:S(2)}) collective-permute-start(bf16[768,640]{1,0:T(8,128)(2,1)S(1)} %get-tuple-element.159.low_a_ref.cols_a_ref), channel_id=1, source_target_pairs={{0,1},{1,0},{2,3},{3,2},{4,5},{5,4},{6,7},{7,6},{8,9},{9,8},{10,11... | collective-permute-start | bytes 2949128 | tf_op jit(solution)/shard_map/ppermute | solution.py:716
  197.2 10.7 %collective-permute-start.38 = (bf16[192,768]{1,0:T(8,128)(2,1)S(1)}, bf16[192,768]{1,0:T(8,128)(2,1)S(1)}, u32[]{:S(2)}, u32[]{:S(2)}) collective-permute-start(bf16[192,768]{1,0:T(8,128)(2,1)S(1)} %fusion.34), channel_id=1, source_target_pairs={{0,8},{1,9},{2,10},{3,11},{4,12},{5,13},{6,14},{7,15},{8,0},{9,1},... | collective-permute-start | bytes 884744 | tf_op jit(solution)/shard_map/ppermute | solution.py:716
  206.0 19.9 %collective-permute-start.36 = (bf16[192,1536]{1,0:T(8,128)(2,1)S(1)}, bf16[192,1536]{1,0:T(8,128)(2,1)S(1)}, u32[]{:S(2)}, u32[]{:S(2)}) collective-permute-start(bf16[192,1536]{1,0:T(8,128)(2,1)S(1)} %get-tuple-element.206), channel_id=1, source_target_pairs={{0,2},{1,3},{2,0},{3,1},{4,6},{5,7},{6,4},{7,5},{8,10},{9,11},{10,... | collective-permute-start | bytes 1769480 | tf_op jit(solution)/shard_map/ppermute | solution.py:716
  207.4 24.6 %collective-permute-start.48 = (bf16[192,1536]{1,0:T(8,128)(2,1)S(1)}, bf16[192,1536]{1,0:T(8,128)(2,1)S(1)}, u32[]{:S(2)}, u32[]{:S(2)}) collective-permute-start(bf16[192,1536]{1,0:T(8,128)(2,1)S(1)} %get-tuple-element.207), channel_id=1, source_target_pairs={{0,4},{1,5},{2,6},{3,7},{4,0},{5,1},{6,2},{7,3},{8,12},{9,13},{10,... | collective-permute-start | bytes 1769480 | tf_op jit(solution)/shard_map/ppermute | solution.py:716
  208.1 17.7 %collective-permute-start.39 = (bf16[96,768]{1,0:T(8,128)(2,1)S(1)}, bf16[96,768]{1,0:T(8,128)(2,1)S(1)}, u32[]{:S(2)}, u32[]{:S(2)}) collective-permute-start(bf16[96,768]{1,0:T(8,128)(2,1)S(1)} %split.41), channel_id=1, source_target_pairs={{0,16},{1,17},{2,18},{3,19},{4,20},{5,21},{6,22},{7,23},{8,24},{9,... | collective-permute-start | bytes 442376 | tf_op jit(solution)/shard_map/ppermute | solution.py:716
  224.4 19.4 %collective-permute-start.42 = (bf16[192,896]{1,0:T(8,128)(2,1)S(1)}, bf16[192,896]{1,0:T(8,128)(2,1)S(1)}, u32[]{:S(2)}, u32[]{:S(2)}) collective-permute-start(bf16[192,896]{1,0:T(8,128)(2,1)S(1)} %get-tuple-element.184), channel_id=1, source_target_pairs={{0,4},{1,5},{2,6},{3,7},{4,0},{5,1},{6,2},{7,3},{8,12},{9,13},{10,... | collective-permute-start | bytes 1032200 | tf_op jit(solution)/shard_map/ppermute | solution.py:716
  225.0 20.2 %collective-permute-start.45 = (bf16[2,192,896]{2,1,0:T(8,128)(2,1)S(1)}, bf16[2,192,896]{2,1,0:T(8,128)(2,1)S(1)}, u32[]{:S(2)}, u32[]{:S(2)}) collective-permute-start(bf16[2,192,896]{2,1,0:T(8,128)(2,1)S(1)} %get-tuple-element.187), channel_id=1, source_target_pairs={{0,2},{1,3},{2,0},{3,1},{4,6},{5,7},{6,4},{7,5},{8,10},{9,11},{10,... | collective-permute-start | bytes 2064392 | tf_op jit(solution)/shard_map/ppermute | solution.py:716
  226.1 13.1 %collective-permute-start.49 = (bf16[192,1536]{1,0:T(8,128)(2,1)S(1)}, bf16[192,1536]{1,0:T(8,128)(2,1)S(1)}, u32[]{:S(2)}, u32[]{:S(2)}) collective-permute-start(bf16[192,1536]{1,0:T(8,128)(2,1)S(1)} %fusion.14), channel_id=1, source_target_pairs={{0,8},{1,9},{2,10},{3,11},{4,12},{5,13},{6,14},{7,15},{8,0},{9,1},... | collective-permute-start | bytes 1769480 | tf_op jit(solution)/shard_map/ppermute | solution.py:716
  230.8 11.1 %collective-permute-start.40 = (bf16[512,768]{1,0:T(8,128)(2,1)S(1)}, bf16[512,768]{1,0:T(8,128)(2,1)S(1)}, u32[]{:S(2)}, u32[]{:S(2)}) collective-permute-start(bf16[512,768]{1,0:T(8,128)(2,1)S(1)} %get-tuple-element.178), channel_id=1, source_target_pairs={{0,1},{1,0},{2,3},{3,2},{4,5},{5,4},{6,7},{7,6},{8,9},{9,8},{10,11... | collective-permute-start | bytes 2359304 | tf_op jit(solution)/shard_map/ppermute | solution.py:716
  232.0 20.8 %collective-permute-start.41 = (bf16[192,896]{1,0:T(8,128)(2,1)S(1)}, bf16[192,896]{1,0:T(8,128)(2,1)S(1)}, u32[]{:S(2)}, u32[]{:S(2)}) collective-permute-start(bf16[192,896]{1,0:T(8,128)(2,1)S(1)} %get-tuple-element.175), channel_id=1, source_target_pairs={{0,4},{1,5},{2,6},{3,7},{4,0},{5,1},{6,2},{7,3},{8,12},{9,13},{10,... | collective-permute-start | bytes 1032200 | tf_op jit(solution)/shard_map/ppermute | solution.py:716
  239.6 13.1 %collective-permute-start.50 = (bf16[96,1536]{1,0:T(8,128)(2,1)S(1)}, bf16[96,1536]{1,0:T(8,128)(2,1)S(1)}, u32[]{:S(2)}, u32[]{:S(2)}) collective-permute-start(bf16[96,1536]{1,0:T(8,128)(2,1)S(1)} %split.39), channel_id=1, source_target_pairs={{0,16},{1,17},{2,18},{3,19},{4,20},{5,21},{6,22},{7,23},{8,24},{9,... | collective-permute-start | bytes 884744 | tf_op jit(solution)/shard_map/ppermute | solution.py:716
  244.0 8.9 %collective-permute-start.43 = (bf16[192,896]{1,0:T(8,128)(2,1)S(1)}, bf16[192,896]{1,0:T(8,128)(2,1)S(1)}, u32[]{:S(2)}, u32[]{:S(2)}) collective-permute-start(bf16[192,896]{1,0:T(8,128)(2,1)S(1)} %add_convert_fusion.3), channel_id=1, source_target_pairs={{0,2},{1,3},{2,0},{3,1},{4,6},{5,7},{6,4},{7,5},{8,10},{9,11},{10,... | collective-permute-start | bytes 1032200 | tf_op jit(solution)/shard_map/ppermute | solution.py:716
  245.4 11.1 %collective-permute-start.46 = (bf16[192,896]{1,0:T(8,128)(2,1)S(1)}, bf16[192,896]{1,0:T(8,128)(2,1)S(1)}, u32[]{:S(2)}, u32[]{:S(2)}) collective-permute-start(bf16[192,896]{1,0:T(8,128)(2,1)S(1)} %fusion.27), channel_id=1, source_target_pairs={{0,4},{1,5},{2,6},{3,7},{4,0},{5,1},{6,2},{7,3},{8,12},{9,13},{10,... | collective-permute-start | bytes 1032200 | tf_op jit(solution)/shard_map/ppermute | solution.py:716
  253.0 9.2 %collective-permute-start.47 = (bf16[192,896]{1,0:T(8,128)(2,1)S(1)}, bf16[192,896]{1,0:T(8,128)(2,1)S(1)}, u32[]{:S(2)}, u32[]{:S(2)}) collective-permute-start(bf16[192,896]{1,0:T(8,128)(2,1)S(1)} %add_convert_fusion.2), channel_id=1, source_target_pairs={{0,8},{1,9},{2,10},{3,11},{4,12},{5,13},{6,14},{7,15},{8,0},{9,1},... | collective-permute-start | bytes 1032200 | tf_op jit(solution)/shard_map/ppermute | solution.py:716
  254.4 10.2 %collective-permute-start.44 = (bf16[256,768]{1,0:T(8,128)(2,1)S(1)}, bf16[256,768]{1,0:T(8,128)(2,1)S(1)}, u32[]{:S(2)}, u32[]{:S(2)}) collective-permute-start(bf16[256,768]{1,0:T(8,128)(2,1)S(1)} %slice.287), channel_id=1, source_target_pairs={{0,2},{1,3},{2,0},{3,1},{4,6},{5,7},{6,4},{7,5},{8,10},{9,11},{10,... | collective-permute-start | bytes 1179656 | tf_op jit(solution)/shard_map/ppermute | solution.py:716
  264.6 9.3 %collective-permute-start.51 = (bf16[96,896]{1,0:T(8,128)(2,1)S(1)}, bf16[96,896]{1,0:T(8,128)(2,1)S(1)}, u32[]{:S(2)}, u32[]{:S(2)}) collective-permute-start(bf16[96,896]{1,0:T(8,128)(2,1)S(1)} %split.40), channel_id=1, source_target_pairs={{0,16},{1,17},{2,18},{3,19},{4,20},{5,21},{6,22},{7,23},{8,24},{9,... | collective-permute-start | bytes 516104 | tf_op jit(solution)/shard_map/ppermute | solution.py:716
  (52 other events, 425.7 us)
where the time goes:
time: 283 us; the launch traced here: 277 us
  Pallas kernels  99.4 us (35%)
  waiting for transfers between devices  88 us (31%)
  starting transfers between devices  51.5 us (18%)
  local copies, waits for them, and re-layouts  18.9 us (7%)
  other arithmetic  10.8 us (4%)
  matrix products  6.47 us (2%)
    ppermute x52, waiting for transfers between devices, send(): return lax.ppermute(v, ('row', 'col'), pairs)  88 us
    ppermute x52, starting transfers between devices, send(): return lax.ppermute(v, ('row', 'col'), pairs)  51.5 us
    pallas_call x2, Pallas kernels, attend_back(): pl.pallas_call(attend_back_kernel, grid_spec=grid_spec, out_shape=[jax.Sh...  28.9 us
    pallas_call x2, Pallas kernels, mlp_back(): pl.pallas_call(functools.partial(mlp_back_kernel, has_base), grid=(2,), i...  21.7 us
    pallas_call x2, Pallas kernels, attend(): pl.pallas_call(attend_kernel, grid_spec=grid_spec, out_shape=[jax.ShapeDt...  15.2 us
    pallas_call x4, Pallas kernels, mlp(): pl.pallas_call(functools.partial(mlp_kernel, has_base), grid=(2,), in_spe...  14.7 us
    unnamed x103, local copies, waits for them, and re-layouts  13.6 us
    pallas_call x2, Pallas kernels, qkv_back(): pl.pallas_call(qkv_back_kernel, grid=(1,), in_specs=[whole(dq.shape), who...  7.93 us
  transfers between devices with their start and end apart: 52, of which 19 were waited for; matrix products, arithmetic and copies ran while one was open for 8% of the time, Pallas kernels for 34%

commit v1 on v0

--- a/solution.py
+++ b/solution.py
@@ -847,9 +847,10 @@
     dy_came = links.across(tie(dy_other.astype(bf16), attn_shard, small_other))
 
     odd = core == 1
-    ring_a = links.ring_gather(attn_shard)
+    grow_a = links.ring_gather(attn_shard, last=1)
+    ring_a = links.ring_grow(grow_a, 0)
     x_a, y_a = links.along(ring_a), links.across(ring_a)
-    ring_b = links.ring_gather(tie(mlp_shards[0], ring_a))
+    ring_b = links.ring_gather(tie(mlp_shards[0], grow_a))
     turn_a = jnp.where(odd, y_a, x_a)
     attn_w = [ring_a, x_a, y_a, links.far(turn_a)]
 
@@ -864,8 +865,9 @@
 
     ring_b = tie(ring_b, turn_a, cosine, sine, qcode, kcode)
     x_b, y_b = links.along(ring_b), links.across(ring_b)
-    ring_c = links.ring_gather(tie(mlp_shards[1], ring_b))
+    grow_c = links.ring_gather(tie(mlp_shards[1], ring_b), last=1)
     q, kv, wo = qkv(tie(x, ring_b, dy_came), x_other, cosine, sine, attn_w)
+    ring_c = links.ring_grow(tie(grow_c, q), 0)
     att_0, logs_0 = attend(first_quarter, q, kv, qcode, kcode)
     att_1, logs_1 = attend(second_quarter, tie(q, att_0), kv, qcode, kcode)
     held_x, held_y = lax.optimization_barrier((x_b, y_b, att_1))[:2]

time: 283 us -> 277 us (0.979)
  starting transfers between devices: 51.5 us -> 44.9 us
    ppermute x52, starting transfers between devices: 51.5 us -> 44.9 us  [send(): return lax.ppermute(v, ('row', 'col'), pairs)]
  transfers between devices with their start and end apart: 52 -> 52, of which waited for: 19 -> 21; matrix products, arithmetic and copies ran while one was open for 8% -> 8% of each run, Pallas kernels for 34% -> 34%
where the time goes in v1:
time: 277 us; the launch traced here: 271 us
  Pallas kernels  99.4 us (36%)
  waiting for transfers between devices  88.5 us (32%)
  starting transfers between devices  44.9 us (16%)
  local copies, waits for them, and re-layouts  18.9 us (7%)
  other arithmetic  10.9 us (4%)
  matrix products  6.48 us (2%)
    ppermute x52, waiting for transfers between devices, send(): return lax.ppermute(v, ('row', 'col'), pairs)  88.5 us
    ppermute x52, starting transfers between devices, send(): return lax.ppermute(v, ('row', 'col'), pairs)  44.9 us
    pallas_call x2, Pallas kernels, attend_back(): pl.pallas_call(attend_back_kernel, grid_spec=grid_spec, out_shape=[jax.Sh...  28.9 us
    pallas_call x2, Pallas kernels, mlp_back(): pl.pallas_call(functools.partial(mlp_back_kernel, has_base), grid=(2,), i...  21.8 us
    pallas_call x2, Pallas kernels, attend(): pl.pallas_call(attend_kernel, grid_spec=grid_spec, out_shape=[jax.ShapeDt...  15.2 us
    pallas_call x4, Pallas kernels, mlp(): pl.pallas_call(functools.partial(mlp_kernel, has_base), grid=(2,), in_spe...  14.7 us
    unnamed x103, local copies, waits for them, and re-layouts  13.7 us
    pallas_call x2, Pallas kernels, qkv_back(): pl.pallas_call(qkv_back_kernel, grid=(1,), in_specs=[whole(dq.shape), who...  7.93 us
  transfers between devices with their start and end apart: 52, of which 21 were waited for; matrix products, arithmetic and copies ran while one was open for 8% of the time, Pallas kernels for 34%

profile of v1, /device:TPU:0, one launch (start us, length us, event | category | flops | bytes accessed | tf_op | source)
XLA Modules:
  0.0 271.2 jit_solution(13596925581657985259)
XLA Ops:
  2.6 4.1 %collective-permute-start.1 = (bf16[96,768]{1,0:T(8,128)(2,1)S(1)}, bf16[96,768]{1,0:T(8,128)(2,1)S(1)}, u32[]{:S(2)}, u32[]{:S(2)}) collective-permute-start(bf16[96,768]{1,0:T(8,128)(2,1)S(1)} %concatenate.57), channel_id=1, source_target_pairs={{0,16},{1,17},{2,18},{3,19},{4,20},{5,21},{6,22},{7,23},{8,24},{9,... | collective-permute-start | bytes 442376 | tf_op jit(solution)/shard_map/ppermute | solution.py:716
  7.6 1.6 collective-permute-start.7
  9.2 2.2 dynamic-slice_bitcast_fusion.2
  11.9 1.5 collective-permute-start.9
  15.5 1.6 collective-permute-start.4
  17.2 1.9 fusion.35
  20.1 6.6 %collective-permute-done.4 = bf16[192,768]{1,0:T(8,128)(2,1)S(1)} collective-permute-done((bf16[192,768]{1,0:T(8,128)(2,1)S(1)}, bf16[192,768]{1,0:T(8,128)(2,1)S(1)}, u32[]{:S(2)}, u32[]{:S(2)}) %collective-permute-start.4) | collective-permute-done | bytes 294944 | tf_op jit(solution)/shard_map/ppermute | solution.py:716
  26.8 1.6 collective-permute-start.5
  28.4 1.5 collective-permute-start.6
  29.9 6.4 %collective-permute-done.2 = bf16[96,1664]{1,0:T(8,128)(2,1)S(1)} collective-permute-done((bf16[96,1664]{1,0:T(8,128)(2,1)S(1)}, bf16[96,1664]{1,0:T(8,128)(2,1)S(1)}, u32[]{:S(2)}, u32[]{:S(2)}) %collective-permute-start.2) | collective-permute-done | bytes 319520 | tf_op jit(solution)/shard_map/ppermute | solution.py:716
  37.6 5.1 %collective-permute-done.5.rest_2_.top_ref = bf16[384,768]{1,0:T(8,128)(2,1)S(1)} collective-permute-done((bf16[384,768]{1,0:T(8,128)(2,1)S(1)}, bf16[384,768]{1,0:T(8,128)(2,1)S(1)}, u32[]{:S(2)}, u32[]{:S(2)}) %collective-permute-start.5) | collective-permute-done | bytes 589856 | tf_op jit(solution)/shard_map/ppermute | solution.py:716
  43.4 8.3 %collective-permute-done.3 = bf16[192,1664]{1,0:T(8,128)(2,1)S(1)} collective-permute-done((bf16[192,1664]{1,0:T(8,128)(2,1)S(1)}, bf16[192,1664]{1,0:T(8,128)(2,1)S(1)}, u32[]{:S(2)}, u32[]{:S(2)}) %collective-permute-start.3) | collective-permute-done | bytes 639008 | tf_op jit(solution)/shard_map/ppermute | solution.py:716
  52.1 1.6 collective-permute-start.12
  54.4 5.5 %collective-permute-done.14 = bf16[96,768]{1,0:T(8,128)(2,1)S(1)} collective-permute-done((bf16[96,768]{1,0:T(8,128)(2,1)S(1)}, bf16[96,768]{1,0:T(8,128)(2,1)S(1)}, u32[]{:S(2)}, u32[]{:S(2)}) %collective-permute-start.14) | collective-permute-done | bytes 147488 | tf_op jit(solution)/shard_map/ppermute | solution.py:716
  60.0 5.3 %qkv.1 = (bf16[1024,512]{1,0:T(8,128)(2,1)S(1)}, bf16[1024,1024]{1,0:T(8,128)(2,1)S(1)}, bf16[768,512]{1,0:T(8,128)(2,1)S(1)}) custom-call(bf16[512,768]{1,0:T(8,128)(2,1)S(1)} %fusion.9.own_ref.x_ref, bf16[512,768]{1,0:T(8,128)(2,1)S(1)} %collective-permute-done.10.other_ref, f32[1024,128]{1,0:T(8,128)S(1)} %get-tuple-element.249.cos_ref, ...), custom_call_target="tpu_custom_call" | custom-call | flops 2415919104 | bytes 7864320 | tf_op jit(solution)/shard_map/qkv/pallas_call | solution.py:131
  65.3 7.6 %attend.2 = (bf16[1024,256]{1,0:T(8,128)(2,1)S(1)}, f32[8,1024]{1,0:T(8,128)S(1)}) custom-call(s32[1]{0:T(128)} %constant.169.clone.1.quarter_ref, bf16[1024,512]{1,0:T(8,128)(2,1)S(1)} %get-tuple-element.170.q_ref, bf16[1024,1024]{1,0:T(8,128)(2,1)S(1)} %get-tuple-element.106.kv_ref, bf16[1024,128]{1,0:T(8,128)(2,1)S(1)} %fusion.37.qcode_ref, ...), custom_call_target="tpu_custom_call" | custom-call | flops 4294967296 | bytes 3145728 | tf_op jit(solution)/shard_map/attend/pallas_call | solution.py:222
  73.0 7.6 %attend.3 = (bf16[1024,256]{1,0:T(8,128)(2,1)S(1)}, f32[8,1024]{1,0:T(8,128)S(1)}) custom-call(s32[1]{0:T(128)} %constant.182.clone.1.quarter_ref, bf16[1024,512]{1,0:T(8,128)(2,1)S(1)} %get-tuple-element.170.q_ref, bf16[1024,1024]{1,0:T(8,128)(2,1)S(1)} %get-tuple-element.106.kv_ref, bf16[1024,128]{1,0:T(8,128)(2,1)S(1)} %fusion.37.qcode_ref, ...), custom_call_target="tpu_custom_call" | custom-call | flops 4294967296 | bytes 3145728 | tf_op jit(solution)/shard_map/attend/pallas_call | solution.py:222
  86.3 1.5 collective-permute-start.22
  89.4 15.9 %collective-permute-done.16.rest_3_.rest_13_ = bf16[384,1664]{1,0:T(8,128)(2,1)S(1)} collective-permute-done((bf16[384,1664]{1,0:T(8,128)(2,1)S(1)}, bf16[384,1664]{1,0:T(8,128)(2,1)S(1)}, u32[]{:S(2)}, u32[]{:S(2)}) %collective-permute-start.16) | collective-permute-done | bytes 1277984 | tf_op jit(solution)/shard_map/ppermute | solution.py:716
  106.3 4.8 %mlp.4 = (bf16[2,3,512,512]{3,2,1,0:T(8,128)(2,1)S(1)}, f32[512,768]{1,0:T(8,128)S(1)}) custom-call(bf16[512,768]{1,0:T(8,128)(2,1)S(1)} %get-tuple-element.133.low_ref, bf16[384,1664]{1,0:T(8,128)(2,1)S(1)} %pad_maximum_fusion.2.norm_a_ref.rest_0_.rest_10_, bf16[384,1664]{1,0:T(8,128)(2,1)S(1)} %collective-permute-done.12.norm_b_ref.rest_1_.rest_11_, ...), custom_call_target="tpu_custom_call" | custom-call | flops 2415919104 | bytes 11796480 | tf_op jit(solution)/shard_map/mlp/pallas_call | solution.py:434
  113.6 4.9 %mlp.5 = (bf16[2,3,512,512]{3,2,1,0:T(8,128)(2,1)S(1)}, f32[512,768]{1,0:T(8,128)S(1)}) custom-call(bf16[512,768]{1,0:T(8,128)(2,1)S(1)} %collective-permute-done.19.low_ref, bf16[384,1664]{1,0:T(8,128)(2,1)S(1)} %pad_maximum_fusion.2.norm_a_ref.rest_0_.rest_10_, bf16[384,1664]{1,0:T(8,128)(2,1)S(1)} %collective-permute-done.12.norm_b_ref.rest_1_.rest_11_, ...), custom_call_target="tpu_custom_call" | custom-call | flops 2415919104 | bytes 11796480 | tf_op jit(solution)/shard_map/mlp/pallas_call | solution.py:434
  118.5 3.2 %collective-permute-done.23.rest_4_.rest_11_ = bf16[384,768]{1,0:T(8,128)(2,1)S(1)} collective-permute-done((bf16[384,768]{1,0:T(8,128)(2,1)S(1)}, bf16[384,768]{1,0:T(8,128)(2,1)S(1)}, u32[]{:S(2)}, u32[]{:S(2)}) %collective-permute-start.23) | collective-permute-done | bytes 589856 | tf_op jit(solution)/shard_map/ppermute | solution.py:716
  121.7 2.5 mlp.6
  124.3 2.5 mlp.7
  126.8 1.7 second_norm.1
  132.1 8.0 %mlp_back.2 = (f32[512,768]{1,0:T(8,128)S(1)}, f32[512,768]{1,0:T(8,128)S(1)}, bf16[2,192,768]{2,1,0:T(8,128)(2,1)S(1)}, bf16[2,192,768]{2,1,0:T(8,128)(2,1)S(1)}, bf16[4,192,768]{2,1,0:T(8,128)(2,1)S(1)}) custom-call(bf16[512,768]{1,0:T(8,128)(2,1)S(1)} %get-tuple-element.137.rest_0_, bf16[512,768]{1,0:T(8,128)(2,1)S(1)} %collective-permute-done.25.rest_1_, ...), custom_call_target="tpu_custom_call" | custom-call | flops 4831838208 | bytes 19660800 | tf_op jit(solution)/shard_map/mlp_back/pallas_call | solution.py:556
  143.1 13.8 %mlp_back.3 = (f32[512,768]{1,0:T(8,128)S(1)}, bf16[512,768]{1,0:T(8,128)(2,1)S(1)}, bf16[2,192,1536]{2,1,0:T(8,128)(2,1)S(1)}, bf16[2,192,1536]{2,1,0:T(8,128)(2,1)S(1)}, bf16[4,192,1536]{2,1,0:T(8,128)(2,1)S(1)}) custom-call(bf16[512,768]{1,0:T(8,128)(2,1)S(1)} %get-tuple-element.137.rest_0_, bf16[512,768]{1,0:T(8,128)(2,1)S(1)} %collective-permute-done.25.rest_1_, ...), custom_call_target="tpu_custom_call" | custom-call | flops 9663676416 | bytes 39321600 | tf_op jit(solution)/shard_map/mlp_back/pallas_call | solution.py:556
  157.1 1.3 fusion.45
  159.3 2.0 first_back.1
  171.9 1.6 copy-done.29
  174.7 14.5 %attend_back.2 = (bf16[1024,256]{1,0:T(8,128)(2,1)S(1)}, bf16[1024,512]{1,0:T(8,128)(2,1)S(1)}) custom-call(s32[1]{0:T(128)} %constant.182.clone.1.quarter_ref, bf16[1024,512]{1,0:T(8,128)(2,1)S(1)} %copy-done.32, bf16[1024,1024]{1,0:T(8,128)(2,1)S(1)} %copy-done.29, bf16[512,768]{1,0:T(8,128)(2,1)} %get-tuple-element.155.own_ref, ...), custom_call_target="tpu_custom_call" | custom-call | flops 10737418240 | bytes 7864320 | tf_op jit(solution)/shard_map/attend_back/pallas_call | solution.py:326
  189.4 1.5 collective-permute-start.38
  191.0 4.1 %qkv_back.2 = (f32[512,768]{1,0:T(8,128)S(1)}, bf16[512,768]{1,0:T(8,128)(2,1)S(1)}, bf16[2,192,896]{2,1,0:T(8,128)(2,1)S(1)}, bf16[192,896]{1,0:T(8,128)(2,1)S(1)}, bf16[192,896]{1,0:T(8,128)(2,1)S(1)}) custom-call(bf16[1024,256]{1,0:T(8,128)(2,1)S(1)} %get-tuple-element.159.dq_ref, bf16[1024,512]{1,0:T(8,128)(2,1)S(1)} %get-tuple-element.160.dkv_ref, ...), custom_call_target="tpu_custom_call" | custom-call | flops 2617245696 | bytes 7864320 | tf_op jit(solution)/shard_map/qkv_back/pallas_call | solution.py:670
  195.1 3.2 %collective-permute-done.35 = bf16[2,192,1536]{2,1,0:T(8,128)(2,1)S(1)} collective-permute-done((bf16[2,192,1536]{2,1,0:T(8,128)(2,1)}, bf16[2,192,1536]{2,1,0:T(8,128)(2,1)S(1)}, u32[]{:S(2)}, u32[]{:S(2)}) %collective-permute-start.35) | collective-permute-done | bytes 1179680 | tf_op jit(solution)/shard_map/ppermute | solution.py:716
  200.5 2.3 collective-permute-start.39
  202.8 14.4 %attend_back.3 = (bf16[1024,256]{1,0:T(8,128)(2,1)S(1)}, bf16[1024,512]{1,0:T(8,128)(2,1)S(1)}) custom-call(s32[1]{0:T(128)} %constant.169.clone.1.quarter_ref, bf16[1024,512]{1,0:T(8,128)(2,1)S(1)} %copy-done.33, bf16[1024,1024]{1,0:T(8,128)(2,1)S(1)} %copy-done.30, bf16[512,768]{1,0:T(8,128)(2,1)} %get-tuple-element.155.own_ref, ...), custom_call_target="tpu_custom_call" | custom-call | flops 10737418240 | bytes 7864320 | tf_op jit(solution)/shard_map/attend_back/pallas_call | solution.py:326
  217.2 1.6 collective-permute-start.42
  218.8 1.3 collective-permute-start.45
  221.1 3.8 %qkv_back.3 = (f32[512,768]{1,0:T(8,128)S(1)}, bf16[512,768]{1,0:T(8,128)(2,1)S(1)}, bf16[2,192,896]{2,1,0:T(8,128)(2,1)S(1)}, bf16[192,896]{1,0:T(8,128)(2,1)S(1)}, bf16[192,896]{1,0:T(8,128)(2,1)S(1)}) custom-call(bf16[1024,256]{1,0:T(8,128)(2,1)S(1)} %get-tuple-element.174.dq_ref, bf16[1024,512]{1,0:T(8,128)(2,1)S(1)} %get-tuple-element.175.dkv_ref, ...), custom_call_target="tpu_custom_call" | custom-call | flops 2617245696 | bytes 7864320 | tf_op jit(solution)/shard_map/qkv_back/pallas_call | solution.py:670
  226.2 1.3 collective-permute-start.41
  227.4 6.0 %collective-permute-done.49 = bf16[192,1536]{1,0:T(8,128)(2,1)S(1)} collective-permute-done((bf16[192,1536]{1,0:T(8,128)(2,1)S(1)}, bf16[192,1536]{1,0:T(8,128)(2,1)S(1)}, u32[]{:S(2)}, u32[]{:S(2)}) %collective-permute-start.49) | collective-permute-done | bytes 589856 | tf_op jit(solution)/shard_map/ppermute | solution.py:716
  237.3 1.4 collective-permute-start.46
  238.6 8.3 %collective-permute-done.50 = bf16[96,1536]{1,0:T(8,128)(2,1)S(1)} collective-permute-done((bf16[96,1536]{1,0:T(8,128)(2,1)S(1)}, bf16[96,1536]{1,0:T(8,128)(2,1)S(1)}, u32[]{:S(2)}, u32[]{:S(2)}) %collective-permute-start.50) | collective-permute-done | bytes 294944 | tf_op jit(solution)/shard_map/ppermute | solution.py:716
  247.4 1.3 copy.36
  250.1 6.2 %collective-permute-done.47 = bf16[192,896]{1,0:T(8,128)(2,1)S(1)} collective-permute-done((bf16[192,896]{1,0:T(8,128)(2,1)S(1)}, bf16[192,896]{1,0:T(8,128)(2,1)S(1)}, u32[]{:S(2)}, u32[]{:S(2)}) %collective-permute-start.47) | collective-permute-done | bytes 344096 | tf_op jit(solution)/shard_map/ppermute | solution.py:716
  256.6 2.2 collective-permute-done.44
  258.8 1.7 collective-permute-start.51
  261.9 6.0 %collective-permute-done.51 = bf16[96,896]{1,0:T(8,128)(2,1)S(1)} collective-permute-done((bf16[96,896]{1,0:T(8,128)(2,1)S(1)}, bf16[96,896]{1,0:T(8,128)(2,1)S(1)}, u32[]{:S(2)}, u32[]{:S(2)}) %collective-permute-start.51) | collective-permute-done | bytes 172064 | tf_op jit(solution)/shard_map/ppermute | solution.py:716
  (256 shorter events, 54.4 us)
Async XLA Ops:
  2.6 12.9 %collective-permute-start.1 = (bf16[96,768]{1,0:T(8,128)(2,1)S(1)}, bf16[96,768]{1,0:T(8,128)(2,1)S(1)}, u32[]{:S(2)}, u32[]{:S(2)}) collective-permute-start(bf16[96,768]{1,0:T(8,128)(2,1)S(1)} %concatenate.57), channel_id=1, source_target_pairs={{0,16},{1,17},{2,18},{3,19},{4,20},{5,21},{6,22},{7,23},{8,24},{9,... | collective-permute-start | bytes 442376 | tf_op jit(solution)/shard_map/ppermute | solution.py:716
  7.6 6.7 %collective-permute-start.7 = (s32[2,256]{1,0:T(2,128)S(1)}, s32[2,256]{1,0:T(2,128)S(1)}, u32[]{:S(2)}, u32[]{:S(2)}) collective-permute-start(s32[2,256]{1,0:T(2,128)S(1)} %bitcast.105), channel_id=1, source_target_pairs={{0,2},{1,3},{2,0},{3,1},{4,6},{5,7},{6,4},{7,5},{8,10},{9,11},{10,... | collective-permute-start | bytes 6152 | tf_op jit(solution)/shard_map/ppermute | solution.py:716
  11.4 25.3 %collective-permute-start = (bf16[256,768]{1,0:T(8,128)(2,1)S(1)}, bf16[256,768]{1,0:T(8,128)(2,1)S(1)}, u32[]{:S(2)}, u32[]{:S(2)}) collective-permute-start(bf16[256,768]{1,0:T(8,128)(2,1)S(1)} %get-tuple-element.100), channel_id=1, source_target_pairs={{0,2},{1,3},{2,0},{3,1},{4,6},{5,7},{6,4},{7,5},{8,10},{9,11},{10,... | collective-permute-start | bytes 1179656 | tf_op jit(solution)/shard_map/ppermute | solution.py:716
  11.9 41.8 %collective-permute-start.9 = (bf16[256,768]{1,0:T(8,128)(2,1)}, bf16[256,768]{1,0:T(8,128)(2,1)S(1)}, u32[]{:S(2)}, u32[]{:S(2)}) collective-permute-start(bf16[256,768]{1,0:T(8,128)(2,1)} %get-tuple-element.103), channel_id=1, source_target_pairs={{0,2},{1,3},{2,0},{3,1},{4,6},{5,7},{6,4},{7,5},{8,10},{9,11},{10,... | collective-permute-start | bytes 1179656 | tf_op jit(solution)/shard_map/ppermute | solution.py:716
  15.5 11.2 %collective-permute-start.4 = (bf16[192,768]{1,0:T(8,128)(2,1)S(1)}, bf16[192,768]{1,0:T(8,128)(2,1)S(1)}, u32[]{:S(2)}, u32[]{:S(2)}) collective-permute-start(bf16[192,768]{1,0:T(8,128)(2,1)S(1)} %pad_maximum_fusion.9), channel_id=1, source_target_pairs={{0,8},{1,9},{2,10},{3,11},{4,12},{5,13},{6,14},{7,15},{8,0},{9,1},... | collective-permute-start | bytes 884744 | tf_op jit(solution)/shard_map/ppermute | solution.py:716
  19.1 17.2 %collective-permute-start.2 = (bf16[96,1664]{1,0:T(8,128)(2,1)S(1)}, bf16[96,1664]{1,0:T(8,128)(2,1)S(1)}, u32[]{:S(2)}, u32[]{:S(2)}) collective-permute-start(bf16[96,1664]{1,0:T(8,128)(2,1)S(1)} %fusion.43), channel_id=1, source_target_pairs={{0,16},{1,17},{2,18},{3,19},{4,20},{5,21},{6,22},{7,23},{8,24},{9,... | collective-permute-start | bytes 958472 | tf_op jit(solution)/shard_map/ppermute | solution.py:716
  26.8 15.9 %collective-permute-start.5 = (bf16[384,768]{1,0:T(8,128)(2,1)S(1)}, bf16[384,768]{1,0:T(8,128)(2,1)S(1)}, u32[]{:S(2)}, u32[]{:S(2)}) collective-permute-start(bf16[384,768]{1,0:T(8,128)(2,1)S(1)} %pad_maximum_fusion.6.rest_0_.top_ref), channel_id=1, source_target_pairs={{0,2},{1,3},{2,0},{3,1},{4,6},{5,7},{6,4},{7,5},{8,10},{9,11},{10,... | collective-permute-start | bytes 1769480 | tf_op jit(solution)/shard_map/ppermute | solution.py:716
  28.4 14.4 %collective-permute-start.6 = (bf16[384,768]{1,0:T(8,128)(2,1)S(1)}, bf16[384,768]{1,0:T(8,128)(2,1)S(1)}, u32[]{:S(2)}, u32[]{:S(2)}) collective-permute-start(bf16[384,768]{1,0:T(8,128)(2,1)S(1)} %pad_maximum_fusion.6.rest_0_.top_ref), channel_id=1, source_target_pairs={{0,4},{1,5},{2,6},{3,7},{4,0},{5,1},{6,2},{7,3},{8,12},{9,13},{10,... | collective-permute-start | bytes 1769480 | tf_op jit(solution)/shard_map/ppermute | solution.py:716
  36.3 15.4 %collective-permute-start.3 = (bf16[192,1664]{1,0:T(8,128)(2,1)S(1)}, bf16[192,1664]{1,0:T(8,128)(2,1)S(1)}, u32[]{:S(2)}, u32[]{:S(2)}) collective-permute-start(bf16[192,1664]{1,0:T(8,128)(2,1)S(1)} %pad_maximum_fusion.5), channel_id=1, source_target_pairs={{0,8},{1,9},{2,10},{3,11},{4,12},{5,13},{6,14},{7,15},{8,0},{9,1},... | collective-permute-start | bytes 1916936 | tf_op jit(solution)/shard_map/ppermute | solution.py:716
  37.5 22.4 %collective-permute-start.10 = (bf16[512,768]{1,0:T(8,128)(2,1)S(1)}, bf16[512,768]{1,0:T(8,128)(2,1)S(1)}, u32[]{:S(2)}, u32[]{:S(2)}) collective-permute-start(bf16[512,768]{1,0:T(8,128)(2,1)S(1)} %fusion.9.own_ref.x_ref), channel_id=1, source_target_pairs={{0,1},{1,0},{2,3},{3,2},{4,5},{5,4},{6,7},{7,6},{8,9},{9,8},{10,11... | collective-permute-start | bytes 2359304 | tf_op jit(solution)/shard_map/ppermute | solution.py:716
  42.8 17.1 %collective-permute-start.11 = (bf16[384,768]{1,0:T(8,128)(2,1)S(1)}, bf16[384,768]{1,0:T(8,128)(2,1)S(1)}, u32[]{:S(2)}, u32[]{:S(2)}) collective-permute-start(bf16[384,768]{1,0:T(8,128)(2,1)S(1)} %broadcast_select_fusion.2), channel_id=1, source_target_pairs={{0,2},{1,5},{2,0},{3,7},{4,6},{5,1},{6,4},{7,3},{8,10},{9,13},{10,... | collective-permute-start | bytes 1769480 | tf_op jit(solution)/shard_map/ppermute | solution.py:716
  51.9 8.0 %collective-permute-start.14 = (bf16[96,768]{1,0:T(8,128)(2,1)S(1)}, bf16[96,768]{1,0:T(8,128)(2,1)S(1)}, u32[]{:S(2)}, u32[]{:S(2)}) collective-permute-start(bf16[96,768]{1,0:T(8,128)(2,1)S(1)} %pad_maximum_fusion.12), channel_id=1, source_target_pairs={{0,16},{1,17},{2,18},{3,19},{4,20},{5,21},{6,22},{7,23},{8,24},{9,... | collective-permute-start | bytes 442376 | tf_op jit(solution)/shard_map/ppermute | solution.py:716
  52.1 28.8 %collective-permute-start.12 = (bf16[384,1664]{1,0:T(8,128)(2,1)S(1)}, bf16[384,1664]{1,0:T(8,128)(2,1)S(1)}, u32[]{:S(2)}, u32[]{:S(2)}) collective-permute-start(bf16[384,1664]{1,0:T(8,128)(2,1)S(1)} %pad_maximum_fusion.2.norm_a_ref.rest_0_.rest_10_), channel_id=1, source_target_pairs={{0,4},{1,5},{2,6},{3,7},{4,0},{5,1},{6,2},{7,3},{8,12},{9,13},{10,... | collective-permute-start | bytes 3833864 | tf_op jit(solution)/shard_map/ppermute | solution.py:716
  53.6 27.8 %collective-permute-start.13 = (bf16[384,1664]{1,0:T(8,128)(2,1)S(1)}, bf16[384,1664]{1,0:T(8,128)(2,1)S(1)}, u32[]{:S(2)}, u32[]{:S(2)}) collective-permute-start(bf16[384,1664]{1,0:T(8,128)(2,1)S(1)} %pad_maximum_fusion.2.norm_a_ref.rest_0_.rest_10_), channel_id=1, source_target_pairs={{0,2},{1,3},{2,0},{3,1},{4,6},{5,7},{6,4},{7,5},{8,10},{9,11},{10,... | collective-permute-start | bytes 3833864 | tf_op jit(solution)/shard_map/ppermute | solution.py:716
  72.9 8.0 %collective-permute-start.15 = (bf16[192,768]{1,0:T(8,128)(2,1)S(1)}, bf16[192,768]{1,0:T(8,128)(2,1)S(1)}, u32[]{:S(2)}, u32[]{:S(2)}) collective-permute-start(bf16[192,768]{1,0:T(8,128)(2,1)S(1)} %pad_maximum_fusion.10), channel_id=1, source_target_pairs={{0,8},{1,9},{2,10},{3,11},{4,12},{5,13},{6,14},{7,15},{8,0},{9,1},... | collective-permute-start | bytes 884744 | tf_op jit(solution)/shard_map/ppermute | solution.py:716
  81.6 23.6 %collective-permute-start.16 = (bf16[384,1664]{1,0:T(8,128)(2,1)S(1)}, bf16[384,1664]{1,0:T(8,128)(2,1)S(1)}, u32[]{:S(2)}, u32[]{:S(2)}) collective-permute-start(bf16[384,1664]{1,0:T(8,128)(2,1)S(1)} %broadcast_select_fusion), channel_id=1, source_target_pairs={{0,2},{1,5},{2,0},{3,7},{4,6},{5,1},{6,4},{7,3},{8,10},{9,13},{10,... | collective-permute-start | bytes 3833864 | tf_op jit(solution)/shard_map/ppermute | solution.py:716
  84.4 4.9 %collective-permute-start.17 = (bf16[768,512]{1,0:T(8,128)(2,1)S(1)}, bf16[768,512]{1,0:T(8,128)(2,1)S(1)}, u32[]{:S(2)}, u32[]{:S(2)}) collective-permute-start(bf16[768,512]{1,0:T(8,128)(2,1)S(1)} %convolution_convert_fusion.x_a_ref), channel_id=1, source_target_pairs={{0,1},{1,0},{2,3},{3,2},{4,5},{5,4},{6,7},{7,6},{8,9},{9,8},{10,11... | collective-permute-start | bytes 2359304 | tf_op jit(solution)/shard_map/ppermute | solution.py:716
  84.5 20.8 %collective-permute-start.18 = (bf16[512,768]{1,0:T(8,128)(2,1)S(1)}, bf16[512,768]{1,0:T(8,128)(2,1)S(1)}, u32[]{:S(2)}, u32[]{:S(2)}) collective-permute-start(bf16[512,768]{1,0:T(8,128)(2,1)S(1)} %get-tuple-element.121), channel_id=1, source_target_pairs={{0,1},{1,0},{2,3},{3,2},{4,5},{5,4},{6,7},{7,6},{8,9},{9,8},{10,11... | collective-permute-start | bytes 2359304 | tf_op jit(solution)/shard_map/ppermute | solution.py:716
  85.7 26.0 %collective-permute-start.21 = (bf16[384,768]{1,0:T(8,128)(2,1)S(1)}, bf16[384,768]{1,0:T(8,128)(2,1)S(1)}, u32[]{:S(2)}, u32[]{:S(2)}) collective-permute-start(bf16[384,768]{1,0:T(8,128)(2,1)S(1)} %pad_maximum_fusion.7.rest_1_.rest_8_), channel_id=1, source_target_pairs={{0,4},{1,5},{2,6},{3,7},{4,0},{5,1},{6,2},{7,3},{8,12},{9,13},{10,... | collective-permute-start | bytes 1769480 | tf_op jit(solution)/shard_map/ppermute | solution.py:716
  86.3 25.3 %collective-permute-start.22 = (bf16[384,768]{1,0:T(8,128)(2,1)S(1)}, bf16[384,768]{1,0:T(8,128)(2,1)S(1)}, u32[]{:S(2)}, u32[]{:S(2)}) collective-permute-start(bf16[384,768]{1,0:T(8,128)(2,1)S(1)} %pad_maximum_fusion.7.rest_1_.rest_8_), channel_id=1, source_target_pairs={{0,2},{1,3},{2,0},{3,1},{4,6},{5,7},{6,4},{7,5},{8,10},{9,11},{10,... | collective-permute-start | bytes 1769480 | tf_op jit(solution)/shard_map/ppermute | solution.py:716
  106.2 6.5 %collective-permute-start.19 = (bf16[512,768]{1,0:T(8,128)(2,1)S(1)}, bf16[512,768]{1,0:T(8,128)(2,1)S(1)}, u32[]{:S(2)}, u32[]{:S(2)}) collective-permute-start(bf16[512,768]{1,0:T(8,128)(2,1)S(1)} %get-tuple-element.133.low_ref), channel_id=1, source_target_pairs={{0,1},{1,0},{2,3},{3,2},{4,5},{5,4},{6,7},{7,6},{8,9},{9,8},{10,11... | collective-permute-start | bytes 2359304 | tf_op jit(solution)/shard_map/ppermute | solution.py:716
  111.8 9.9 %collective-permute-start.23 = (bf16[384,768]{1,0:T(8,128)(2,1)S(1)}, bf16[384,768]{1,0:T(8,128)(2,1)S(1)}, u32[]{:S(2)}, u32[]{:S(2)}) collective-permute-start(bf16[384,768]{1,0:T(8,128)(2,1)S(1)} %broadcast_select_fusion.1), channel_id=1, source_target_pairs={{0,2},{1,5},{2,0},{3,7},{4,6},{5,1},{6,4},{7,3},{8,10},{9,13},{10,... | collective-permute-start | bytes 1769480 | tf_op jit(solution)/shard_map/ppermute | solution.py:716
  128.5 3.1 %collective-permute-start.25 = (bf16[512,768]{1,0:T(8,128)(2,1)S(1)}, bf16[512,768]{1,0:T(8,128)(2,1)S(1)}, u32[]{:S(2)}, u32[]{:S(2)}) collective-permute-start(bf16[512,768]{1,0:T(8,128)(2,1)S(1)} %get-tuple-element.137.rest_0_), channel_id=1, source_target_pairs={{0,1},{1,0},{2,3},{3,2},{4,5},{5,4},{6,7},{7,6},{8,9},{9,8},{10,11... | collective-permute-start | bytes 2359304 | tf_op jit(solution)/shard_map/ppermute | solution.py:716
  129.0 3.0 %collective-permute-start.26 = (bf16[768,512]{1,0:T(8,128)(2,1)S(1)}, bf16[768,512]{1,0:T(8,128)(2,1)S(1)}, u32[]{:S(2)}, u32[]{:S(2)}) collective-permute-start(bf16[768,512]{1,0:T(8,128)(2,1)S(1)} %get-tuple-element.138.rest_2_), channel_id=1, source_target_pairs={{0,1},{1,0},{2,3},{3,2},{4,5},{5,4},{6,7},{7,6},{8,9},{9,8},{10,11... | collective-permute-start | bytes 2359304 | tf_op jit(solution)/shard_map/ppermute | solution.py:716
  130.8 11.5 %collective-permute-start.27 = (bf16[256,768]{1,0:T(8,128)(2,1)S(1)}, bf16[256,768]{1,0:T(8,128)(2,1)S(1)}, u32[]{:S(2)}, u32[]{:S(2)}) collective-permute-start(bf16[256,768]{1,0:T(8,128)(2,1)S(1)} %get-tuple-element.217), channel_id=1, source_target_pairs={{0,2},{1,3},{2,0},{3,1},{4,6},{5,7},{6,4},{7,5},{8,10},{9,11},{10,... | collective-permute-start | bytes 1179656 | tf_op jit(solution)/shard_map/ppermute | solution.py:716
  140.1 16.9 %collective-permute-start.29 = (bf16[2,192,768]{2,1,0:T(8,128)(2,1)S(1)}, bf16[2,192,768]{2,1,0:T(8,128)(2,1)S(1)}, u32[]{:S(2)}, u32[]{:S(2)}) collective-permute-start(bf16[2,192,768]{2,1,0:T(8,128)(2,1)S(1)} %get-tuple-element.150), channel_id=1, source_target_pairs={{0,4},{1,5},{2,6},{3,7},{4,0},{5,1},{6,2},{7,3},{8,12},{9,13},{10,... | collective-permute-start | bytes 1769480 | tf_op jit(solution)/shard_map/ppermute | solution.py:716
  142.2 14.9 %collective-permute-start.28 = (bf16[2,192,768]{2,1,0:T(8,128)(2,1)S(1)}, bf16[2,192,768]{2,1,0:T(8,128)(2,1)S(1)}, u32[]{:S(2)}, u32[]{:S(2)}) collective-permute-start(bf16[2,192,768]{2,1,0:T(8,128)(2,1)S(1)} %get-tuple-element.149), channel_id=1, source_target_pairs={{0,2},{1,3},{2,0},{3,1},{4,6},{5,7},{6,4},{7,5},{8,10},{9,11},{10,... | collective-permute-start | bytes 1769480 | tf_op jit(solution)/shard_map/ppermute | solution.py:716
  162.4 4.2 %collective-permute-start.31 = (bf16[512,768]{1,0:T(8,128)(2,1)}, bf16[512,768]{1,0:T(8,128)(2,1)}, u32[]{:S(2)}, u32[]{:S(2)}) collective-permute-start(bf16[512,768]{1,0:T(8,128)(2,1)} %get-tuple-element.155.own_ref), channel_id=1, source_target_pairs={{0,1},{1,0},{2,3},{3,2},{4,5},{5,4},{6,7},{7,6},{8,9},{9,8},{10,11... | collective-permute-start | bytes 2359304 | tf_op jit(solution)/shard_map/ppermute | solution.py:716
  162.6 26.6 %collective-permute-start.32 = (bf16[192,768]{1,0:T(8,128)(2,1)}, bf16[192,768]{1,0:T(8,128)(2,1)S(1)}, u32[]{:S(2)}, u32[]{:S(2)}) collective-permute-start(bf16[192,768]{1,0:T(8,128)(2,1)} %get-tuple-element.212), channel_id=1, source_target_pairs={{0,2},{1,3},{2,0},{3,1},{4,6},{5,7},{6,4},{7,5},{8,10},{9,11},{10,... | collective-permute-start | bytes 884744 | tf_op jit(solution)/shard_map/ppermute | solution.py:716
  163.8 36.6 %collective-permute-start.37 = (bf16[192,768]{1,0:T(8,128)(2,1)}, bf16[192,768]{1,0:T(8,128)(2,1)S(1)}, u32[]{:S(2)}, u32[]{:S(2)}) collective-permute-start(bf16[192,768]{1,0:T(8,128)(2,1)} %get-tuple-element.213), channel_id=1, source_target_pairs={{0,4},{1,5},{2,6},{3,7},{4,0},{5,1},{6,2},{7,3},{8,12},{9,13},{10,... | collective-permute-start | bytes 884744 | tf_op jit(solution)/shard_map/ppermute | solution.py:716
  164.7 33.6 %collective-permute-start.35 = (bf16[2,192,1536]{2,1,0:T(8,128)(2,1)}, bf16[2,192,1536]{2,1,0:T(8,128)(2,1)S(1)}, u32[]{:S(2)}, u32[]{:S(2)}) collective-permute-start(bf16[2,192,1536]{2,1,0:T(8,128)(2,1)} %copy-done.24), channel_id=1, source_target_pairs={{0,4},{1,5},{2,6},{3,7},{4,0},{5,1},{6,2},{7,3},{8,12},{9,13},{10,... | collective-permute-start | bytes 3538952 | tf_op jit(solution)/shard_map/ppermute | solution.py:716
  165.8 32.5 %collective-permute-start.34 = (bf16[2,192,1536]{2,1,0:T(8,128)(2,1)}, bf16[2,192,1536]{2,1,0:T(8,128)(2,1)S(1)}, u32[]{:S(2)}, u32[]{:S(2)}) collective-permute-start(bf16[2,192,1536]{2,1,0:T(8,128)(2,1)} %copy-done.23), channel_id=1, source_target_pairs={{0,2},{1,3},{2,0},{3,1},{4,6},{5,7},{6,4},{7,5},{8,10},{9,11},{10,... | collective-permute-start | bytes 3538952 | tf_op jit(solution)/shard_map/ppermute | solution.py:716
  166.7 24.2 %collective-permute-start.33 = (bf16[768,640]{1,0:T(8,128)(2,1)S(1)}, bf16[768,640]{1,0:T(8,128)(2,1)S(1)}, u32[]{:S(2)}, u32[]{:S(2)}) collective-permute-start(bf16[768,640]{1,0:T(8,128)(2,1)S(1)} %get-tuple-element.161.low_a_ref.cols_a_ref), channel_id=1, source_target_pairs={{0,1},{1,0},{2,3},{3,2},{4,5},{5,4},{6,7},{7,6},{8,9},{9,8},{10,11... | collective-permute-start | bytes 2949128 | tf_op jit(solution)/shard_map/ppermute | solution.py:716
  189.4 10.9 %collective-permute-start.38 = (bf16[192,768]{1,0:T(8,128)(2,1)S(1)}, bf16[192,768]{1,0:T(8,128)(2,1)S(1)}, u32[]{:S(2)}, u32[]{:S(2)}) collective-permute-start(bf16[192,768]{1,0:T(8,128)(2,1)S(1)} %fusion.34), channel_id=1, source_target_pairs={{0,8},{1,9},{2,10},{3,11},{4,12},{5,13},{6,14},{7,15},{8,0},{9,1},... | collective-permute-start | bytes 884744 | tf_op jit(solution)/shard_map/ppermute | solution.py:716
  198.6 21.5 %collective-permute-start.36 = (bf16[192,1536]{1,0:T(8,128)(2,1)S(1)}, bf16[192,1536]{1,0:T(8,128)(2,1)S(1)}, u32[]{:S(2)}, u32[]{:S(2)}) collective-permute-start(bf16[192,1536]{1,0:T(8,128)(2,1)S(1)} %get-tuple-element.208), channel_id=1, source_target_pairs={{0,2},{1,3},{2,0},{3,1},{4,6},{5,7},{6,4},{7,5},{8,10},{9,11},{10,... | collective-permute-start | bytes 1769480 | tf_op jit(solution)/shard_map/ppermute | solution.py:716
  199.5 26.7 %collective-permute-start.48 = (bf16[192,1536]{1,0:T(8,128)(2,1)S(1)}, bf16[192,1536]{1,0:T(8,128)(2,1)S(1)}, u32[]{:S(2)}, u32[]{:S(2)}) collective-permute-start(bf16[192,1536]{1,0:T(8,128)(2,1)S(1)} %get-tuple-element.209), channel_id=1, source_target_pairs={{0,4},{1,5},{2,6},{3,7},{4,0},{5,1},{6,2},{7,3},{8,12},{9,13},{10,... | collective-permute-start | bytes 1769480 | tf_op jit(solution)/shard_map/ppermute | solution.py:716
  200.5 19.5 %collective-permute-start.39 = (bf16[96,768]{1,0:T(8,128)(2,1)S(1)}, bf16[96,768]{1,0:T(8,128)(2,1)S(1)}, u32[]{:S(2)}, u32[]{:S(2)}) collective-permute-start(bf16[96,768]{1,0:T(8,128)(2,1)S(1)} %split.41), channel_id=1, source_target_pairs={{0,16},{1,17},{2,18},{3,19},{4,20},{5,21},{6,22},{7,23},{8,24},{9,... | collective-permute-start | bytes 442376 | tf_op jit(solution)/shard_map/ppermute | solution.py:716
  217.2 18.9 %collective-permute-start.42 = (bf16[192,896]{1,0:T(8,128)(2,1)S(1)}, bf16[192,896]{1,0:T(8,128)(2,1)S(1)}, u32[]{:S(2)}, u32[]{:S(2)}) collective-permute-start(bf16[192,896]{1,0:T(8,128)(2,1)S(1)} %get-tuple-element.186), channel_id=1, source_target_pairs={{0,4},{1,5},{2,6},{3,7},{4,0},{5,1},{6,2},{7,3},{8,12},{9,13},{10,... | collective-permute-start | bytes 1032200 | tf_op jit(solution)/shard_map/ppermute | solution.py:716
  218.8 18.4 %collective-permute-start.45 = (bf16[2,192,896]{2,1,0:T(8,128)(2,1)S(1)}, bf16[2,192,896]{2,1,0:T(8,128)(2,1)S(1)}, u32[]{:S(2)}, u32[]{:S(2)}) collective-permute-start(bf16[2,192,896]{2,1,0:T(8,128)(2,1)S(1)} %get-tuple-element.189), channel_id=1, source_target_pairs={{0,2},{1,3},{2,0},{3,1},{4,6},{5,7},{6,4},{7,5},{8,10},{9,11},{10,... | collective-permute-start | bytes 2064392 | tf_op jit(solution)/shard_map/ppermute | solution.py:716
  220.3 13.1 %collective-permute-start.49 = (bf16[192,1536]{1,0:T(8,128)(2,1)S(1)}, bf16[192,1536]{1,0:T(8,128)(2,1)S(1)}, u32[]{:S(2)}, u32[]{:S(2)}) collective-permute-start(bf16[192,1536]{1,0:T(8,128)(2,1)S(1)} %fusion.14), channel_id=1, source_target_pairs={{0,8},{1,9},{2,10},{3,11},{4,12},{5,13},{6,14},{7,15},{8,0},{9,1},... | collective-permute-start | bytes 1769480 | tf_op jit(solution)/shard_map/ppermute | solution.py:716
  225.0 9.2 %collective-permute-start.40 = (bf16[512,768]{1,0:T(8,128)(2,1)S(1)}, bf16[512,768]{1,0:T(8,128)(2,1)S(1)}, u32[]{:S(2)}, u32[]{:S(2)}) collective-permute-start(bf16[512,768]{1,0:T(8,128)(2,1)S(1)} %get-tuple-element.180), channel_id=1, source_target_pairs={{0,1},{1,0},{2,3},{3,2},{4,5},{5,4},{6,7},{7,6},{8,9},{9,8},{10,11... | collective-permute-start | bytes 2359304 | tf_op jit(solution)/shard_map/ppermute | solution.py:716
  226.2 20.9 %collective-permute-start.41 = (bf16[192,896]{1,0:T(8,128)(2,1)S(1)}, bf16[192,896]{1,0:T(8,128)(2,1)S(1)}, u32[]{:S(2)}, u32[]{:S(2)}) collective-permute-start(bf16[192,896]{1,0:T(8,128)(2,1)S(1)} %get-tuple-element.177), channel_id=1, source_target_pairs={{0,4},{1,5},{2,6},{3,7},{4,0},{5,1},{6,2},{7,3},{8,12},{9,13},{10,... | collective-permute-start | bytes 1032200 | tf_op jit(solution)/shard_map/ppermute | solution.py:716
  233.8 13.1 %collective-permute-start.50 = (bf16[96,1536]{1,0:T(8,128)(2,1)S(1)}, bf16[96,1536]{1,0:T(8,128)(2,1)S(1)}, u32[]{:S(2)}, u32[]{:S(2)}) collective-permute-start(bf16[96,1536]{1,0:T(8,128)(2,1)S(1)} %split.39), channel_id=1, source_target_pairs={{0,16},{1,17},{2,18},{3,19},{4,20},{5,21},{6,22},{7,23},{8,24},{9,... | collective-permute-start | bytes 884744 | tf_op jit(solution)/shard_map/ppermute | solution.py:716
  236.2 10.8 %collective-permute-start.43 = (bf16[192,896]{1,0:T(8,128)(2,1)S(1)}, bf16[192,896]{1,0:T(8,128)(2,1)S(1)}, u32[]{:S(2)}, u32[]{:S(2)}) collective-permute-start(bf16[192,896]{1,0:T(8,128)(2,1)S(1)} %add_convert_fusion.3), channel_id=1, source_target_pairs={{0,2},{1,3},{2,0},{3,1},{4,6},{5,7},{6,4},{7,5},{8,10},{9,11},{10,... | collective-permute-start | bytes 1032200 | tf_op jit(solution)/shard_map/ppermute | solution.py:716
  237.3 12.9 %collective-permute-start.46 = (bf16[192,896]{1,0:T(8,128)(2,1)S(1)}, bf16[192,896]{1,0:T(8,128)(2,1)S(1)}, u32[]{:S(2)}, u32[]{:S(2)}) collective-permute-start(bf16[192,896]{1,0:T(8,128)(2,1)S(1)} %fusion.27), channel_id=1, source_target_pairs={{0,4},{1,5},{2,6},{3,7},{4,0},{5,1},{6,2},{7,3},{8,12},{9,13},{10,... | collective-permute-start | bytes 1032200 | tf_op jit(solution)/shard_map/ppermute | solution.py:716
  247.2 9.2 %collective-permute-start.47 = (bf16[192,896]{1,0:T(8,128)(2,1)S(1)}, bf16[192,896]{1,0:T(8,128)(2,1)S(1)}, u32[]{:S(2)}, u32[]{:S(2)}) collective-permute-start(bf16[192,896]{1,0:T(8,128)(2,1)S(1)} %add_convert_fusion.2), channel_id=1, source_target_pairs={{0,8},{1,9},{2,10},{3,11},{4,12},{5,13},{6,14},{7,15},{8,0},{9,1},... | collective-permute-start | bytes 1032200 | tf_op jit(solution)/shard_map/ppermute | solution.py:716
  248.7 10.2 %collective-permute-start.44 = (bf16[256,768]{1,0:T(8,128)(2,1)S(1)}, bf16[256,768]{1,0:T(8,128)(2,1)S(1)}, u32[]{:S(2)}, u32[]{:S(2)}) collective-permute-start(bf16[256,768]{1,0:T(8,128)(2,1)S(1)} %slice.287), channel_id=1, source_target_pairs={{0,2},{1,3},{2,0},{3,1},{4,6},{5,7},{6,4},{7,5},{8,10},{9,11},{10,... | collective-permute-start | bytes 1179656 | tf_op jit(solution)/shard_map/ppermute | solution.py:716
  258.8 9.1 %collective-permute-start.51 = (bf16[96,896]{1,0:T(8,128)(2,1)S(1)}, bf16[96,896]{1,0:T(8,128)(2,1)S(1)}, u32[]{:S(2)}, u32[]{:S(2)}) collective-permute-start(bf16[96,896]{1,0:T(8,128)(2,1)S(1)} %split.40), channel_id=1, source_target_pairs={{0,16},{1,17},{2,18},{3,19},{4,20},{5,21},{6,22},{7,23},{8,24},{9,... | collective-permute-start | bytes 516104 | tf_op jit(solution)/shard_map/ppermute | solution.py:716
  (52 other events, 400.9 us)

commit v2 on v1

--- a/solution.py
+++ b/solution.py
@@ -331,7 +331,7 @@
             jax.ShapeDtypeStruct((rows, 2 * part), bf16),
         ],
         cost_estimate=cost(40 * rows * rows * part, 30 * rows * part, rows * rows * 3),
-        compiler_params=pltpu.CompilerParams(vmem_limit_bytes=22 << 20),
+        compiler_params=pltpu.CompilerParams(vmem_limit_bytes=14 << 20),
         name="attend_back",
     )(quarter, q, kv, own, other, wo, att, logs, qcode, kcode, cosine, sine)
 

time: 277 us -> 277 us (level)
    unnamed x103 -> x107, local copies, waits for them, and re-layouts: 13.7 us -> 13.7 us
where the time goes in v2:
time: 277 us; the launch traced here: 271 us
  Pallas kernels  99.6 us (36%)
  waiting for transfers between devices  88.8 us (32%)
  starting transfers between devices  44.6 us (16%)
  local copies, waits for them, and re-layouts  18.9 us (7%)
  other arithmetic  10.8 us (4%)
  matrix products  6.46 us (2%)
    ppermute x52, waiting for transfers between devices, send(): return lax.ppermute(v, ('row', 'col'), pairs)  88.8 us
    ppermute x52, starting transfers between devices, send(): return lax.ppermute(v, ('row', 'col'), pairs)  44.6 us
    pallas_call x2, Pallas kernels, attend_back(): pl.pallas_call(attend_back_kernel, grid_spec=grid_spec, out_shape=[jax.Sh...  29 us
    pallas_call x2, Pallas kernels, mlp_back(): pl.pallas_call(functools.partial(mlp_back_kernel, has_base), grid=(2,), i...  21.8 us
    pallas_call x2, Pallas kernels, attend(): pl.pallas_call(attend_kernel, grid_spec=grid_spec, out_shape=[jax.ShapeDt...  15.2 us
    pallas_call x4, Pallas kernels, mlp(): pl.pallas_call(functools.partial(mlp_kernel, has_base), grid=(2,), in_spe...  14.7 us
    unnamed x107, local copies, waits for them, and re-layouts  13.7 us
    pallas_call x2, Pallas kernels, qkv_back(): pl.pallas_call(qkv_back_kernel, grid=(1,), in_specs=[whole(dq.shape), who...  7.94 us
  transfers between devices with their start and end apart: 52, of which 21 were waited for; matrix products, arithmetic and copies ran while one was open for 8% of the time, Pallas kernels for 34%

profile of v2, /device:TPU:0, one launch (start us, length us, event | category | flops | bytes accessed | tf_op | source)
XLA Modules:
  0.0 271.3 jit_solution(4949119645557509621)
XLA Ops:
  2.6 4.1 %collective-permute-start.1 = (bf16[96,768]{1,0:T(8,128)(2,1)S(1)}, bf16[96,768]{1,0:T(8,128)(2,1)S(1)}, u32[]{:S(2)}, u32[]{:S(2)}) collective-permute-start(bf16[96,768]{1,0:T(8,128)(2,1)S(1)} %concatenate.57), channel_id=1, source_target_pairs={{0,16},{1,17},{2,18},{3,19},{4,20},{5,21},{6,22},{7,23},{8,24},{9,... | collective-permute-start | bytes 442376 | tf_op jit(solution)/shard_map/ppermute | solution.py:716
  7.6 1.6 collective-permute-start.7
  9.2 2.2 dynamic-slice_bitcast_fusion.2
  11.9 1.5 collective-permute-start.9
  15.5 1.6 collective-permute-start.4
  17.2 1.9 fusion.35
  20.1 6.6 %collective-permute-done.4 = bf16[192,768]{1,0:T(8,128)(2,1)S(1)} collective-permute-done((bf16[192,768]{1,0:T(8,128)(2,1)S(1)}, bf16[192,768]{1,0:T(8,128)(2,1)S(1)}, u32[]{:S(2)}, u32[]{:S(2)}) %collective-permute-start.4) | collective-permute-done | bytes 294944 | tf_op jit(solution)/shard_map/ppermute | solution.py:716
  26.8 1.6 collective-permute-start.5
  28.4 1.5 collective-permute-start.6
  29.9 6.4 %collective-permute-done.2 = bf16[96,1664]{1,0:T(8,128)(2,1)S(1)} collective-permute-done((bf16[96,1664]{1,0:T(8,128)(2,1)S(1)}, bf16[96,1664]{1,0:T(8,128)(2,1)S(1)}, u32[]{:S(2)}, u32[]{:S(2)}) %collective-permute-start.2) | collective-permute-done | bytes 319520 | tf_op jit(solution)/shard_map/ppermute | solution.py:716
  37.6 5.1 %collective-permute-done.5.rest_2_.top_ref = bf16[384,768]{1,0:T(8,128)(2,1)S(1)} collective-permute-done((bf16[384,768]{1,0:T(8,128)(2,1)S(1)}, bf16[384,768]{1,0:T(8,128)(2,1)S(1)}, u32[]{:S(2)}, u32[]{:S(2)}) %collective-permute-start.5) | collective-permute-done | bytes 589856 | tf_op jit(solution)/shard_map/ppermute | solution.py:716
  43.4 8.3 %collective-permute-done.3 = bf16[192,1664]{1,0:T(8,128)(2,1)S(1)} collective-permute-done((bf16[192,1664]{1,0:T(8,128)(2,1)S(1)}, bf16[192,1664]{1,0:T(8,128)(2,1)S(1)}, u32[]{:S(2)}, u32[]{:S(2)}) %collective-permute-start.3) | collective-permute-done | bytes 639008 | tf_op jit(solution)/shard_map/ppermute | solution.py:716
  52.1 1.6 collective-permute-start.12
  54.4 5.5 %collective-permute-done.14 = bf16[96,768]{1,0:T(8,128)(2,1)S(1)} collective-permute-done((bf16[96,768]{1,0:T(8,128)(2,1)S(1)}, bf16[96,768]{1,0:T(8,128)(2,1)S(1)}, u32[]{:S(2)}, u32[]{:S(2)}) %collective-permute-start.14) | collective-permute-done | bytes 147488 | tf_op jit(solution)/shard_map/ppermute | solution.py:716
  60.0 5.3 %qkv.1 = (bf16[1024,512]{1,0:T(8,128)(2,1)S(1)}, bf16[1024,1024]{1,0:T(8,128)(2,1)S(1)}, bf16[768,512]{1,0:T(8,128)(2,1)S(1)}) custom-call(bf16[512,768]{1,0:T(8,128)(2,1)S(1)} %fusion.9.own_ref.x_ref, bf16[512,768]{1,0:T(8,128)(2,1)S(1)} %collective-permute-done.10.other_ref, f32[1024,128]{1,0:T(8,128)S(1)} %get-tuple-element.249.cos_ref, ...), custom_call_target="tpu_custom_call" | custom-call | flops 2415919104 | bytes 7864320 | tf_op jit(solution)/shard_map/qkv/pallas_call | solution.py:131
  65.3 7.6 %attend.2 = (bf16[1024,256]{1,0:T(8,128)(2,1)S(1)}, f32[8,1024]{1,0:T(8,128)S(1)}) custom-call(s32[1]{0:T(128)} %constant.169.clone.1.quarter_ref, bf16[1024,512]{1,0:T(8,128)(2,1)S(1)} %get-tuple-element.170.q_ref, bf16[1024,1024]{1,0:T(8,128)(2,1)S(1)} %get-tuple-element.106.kv_ref, bf16[1024,128]{1,0:T(8,128)(2,1)S(1)} %fusion.37.qcode_ref, ...), custom_call_target="tpu_custom_call" | custom-call | flops 4294967296 | bytes 3145728 | tf_op jit(solution)/shard_map/attend/pallas_call | solution.py:222
  73.0 7.6 %attend.3 = (bf16[1024,256]{1,0:T(8,128)(2,1)S(1)}, f32[8,1024]{1,0:T(8,128)S(1)}) custom-call(s32[1]{0:T(128)} %constant.182.clone.1.quarter_ref, bf16[1024,512]{1,0:T(8,128)(2,1)S(1)} %get-tuple-element.170.q_ref, bf16[1024,1024]{1,0:T(8,128)(2,1)S(1)} %get-tuple-element.106.kv_ref, bf16[1024,128]{1,0:T(8,128)(2,1)S(1)} %fusion.37.qcode_ref, ...), custom_call_target="tpu_custom_call" | custom-call | flops 4294967296 | bytes 3145728 | tf_op jit(solution)/shard_map/attend/pallas_call | solution.py:222
  86.3 1.5 collective-permute-start.22
  89.4 15.9 %collective-permute-done.16.rest_3_.rest_13_ = bf16[384,1664]{1,0:T(8,128)(2,1)S(1)} collective-permute-done((bf16[384,1664]{1,0:T(8,128)(2,1)S(1)}, bf16[384,1664]{1,0:T(8,128)(2,1)S(1)}, u32[]{:S(2)}, u32[]{:S(2)}) %collective-permute-start.16) | collective-permute-done | bytes 1277984 | tf_op jit(solution)/shard_map/ppermute | solution.py:716
  106.3 4.8 %mlp.4 = (bf16[2,3,512,512]{3,2,1,0:T(8,128)(2,1)S(1)}, f32[512,768]{1,0:T(8,128)S(1)}) custom-call(bf16[512,768]{1,0:T(8,128)(2,1)S(1)} %get-tuple-element.133.low_ref, bf16[384,1664]{1,0:T(8,128)(2,1)S(1)} %pad_maximum_fusion.2.norm_a_ref.rest_0_.rest_10_, bf16[384,1664]{1,0:T(8,128)(2,1)S(1)} %collective-permute-done.12.norm_b_ref.rest_1_.rest_11_, ...), custom_call_target="tpu_custom_call" | custom-call | flops 2415919104 | bytes 11796480 | tf_op jit(solution)/shard_map/mlp/pallas_call | solution.py:434
  113.6 4.9 %mlp.5 = (bf16[2,3,512,512]{3,2,1,0:T(8,128)(2,1)S(1)}, f32[512,768]{1,0:T(8,128)S(1)}) custom-call(bf16[512,768]{1,0:T(8,128)(2,1)S(1)} %collective-permute-done.19.low_ref, bf16[384,1664]{1,0:T(8,128)(2,1)S(1)} %pad_maximum_fusion.2.norm_a_ref.rest_0_.rest_10_, bf16[384,1664]{1,0:T(8,128)(2,1)S(1)} %collective-permute-done.12.norm_b_ref.rest_1_.rest_11_, ...), custom_call_target="tpu_custom_call" | custom-call | flops 2415919104 | bytes 11796480 | tf_op jit(solution)/shard_map/mlp/pallas_call | solution.py:434
  118.5 3.2 %collective-permute-done.23.rest_4_.rest_11_ = bf16[384,768]{1,0:T(8,128)(2,1)S(1)} collective-permute-done((bf16[384,768]{1,0:T(8,128)(2,1)S(1)}, bf16[384,768]{1,0:T(8,128)(2,1)S(1)}, u32[]{:S(2)}, u32[]{:S(2)}) %collective-permute-start.23) | collective-permute-done | bytes 589856 | tf_op jit(solution)/shard_map/ppermute | solution.py:716
  121.7 2.5 mlp.6
  124.3 2.5 mlp.7
  126.8 1.7 second_norm.1
  132.1 8.0 %mlp_back.2 = (f32[512,768]{1,0:T(8,128)S(1)}, f32[512,768]{1,0:T(8,128)S(1)}, bf16[2,192,768]{2,1,0:T(8,128)(2,1)S(1)}, bf16[2,192,768]{2,1,0:T(8,128)(2,1)S(1)}, bf16[4,192,768]{2,1,0:T(8,128)(2,1)S(1)}) custom-call(bf16[512,768]{1,0:T(8,128)(2,1)S(1)} %get-tuple-element.137.rest_0_, bf16[512,768]{1,0:T(8,128)(2,1)S(1)} %collective-permute-done.25.rest_1_, ...), custom_call_target="tpu_custom_call" | custom-call | flops 4831838208 | bytes 19660800 | tf_op jit(solution)/shard_map/mlp_back/pallas_call | solution.py:556
  143.1 13.8 %mlp_back.3 = (f32[512,768]{1,0:T(8,128)S(1)}, bf16[512,768]{1,0:T(8,128)(2,1)S(1)}, bf16[2,192,1536]{2,1,0:T(8,128)(2,1)S(1)}, bf16[2,192,1536]{2,1,0:T(8,128)(2,1)S(1)}, bf16[4,192,1536]{2,1,0:T(8,128)(2,1)S(1)}) custom-call(bf16[512,768]{1,0:T(8,128)(2,1)S(1)} %get-tuple-element.137.rest_0_, bf16[512,768]{1,0:T(8,128)(2,1)S(1)} %collective-permute-done.25.rest_1_, ...), custom_call_target="tpu_custom_call" | custom-call | flops 9663676416 | bytes 39321600 | tf_op jit(solution)/shard_map/mlp_back/pallas_call | solution.py:556
  157.1 1.3 fusion.45
  159.3 2.0 first_back.1
  171.9 1.6 copy-done.31
  174.7 14.6 %attend_back.2 = (bf16[1024,256]{1,0:T(8,128)(2,1)S(1)}, bf16[1024,512]{1,0:T(8,128)(2,1)S(1)}) custom-call(s32[1]{0:T(128)} %constant.182.clone.1.quarter_ref, bf16[1024,512]{1,0:T(8,128)(2,1)S(1)} %copy-done.34, bf16[1024,1024]{1,0:T(8,128)(2,1)S(1)} %copy-done.31, bf16[512,768]{1,0:T(8,128)(2,1)} %get-tuple-element.155.own_ref, ...), custom_call_target="tpu_custom_call" | custom-call | flops 10737418240 | bytes 7864320 | tf_op jit(solution)/shard_map/attend_back/pallas_call | solution.py:326
  189.4 1.5 collective-permute-start.38
  191.1 4.1 %qkv_back.2 = (f32[512,768]{1,0:T(8,128)S(1)}, bf16[512,768]{1,0:T(8,128)(2,1)S(1)}, bf16[2,192,896]{2,1,0:T(8,128)(2,1)S(1)}, bf16[192,896]{1,0:T(8,128)(2,1)S(1)}, bf16[192,896]{1,0:T(8,128)(2,1)S(1)}) custom-call(bf16[1024,256]{1,0:T(8,128)(2,1)S(1)} %get-tuple-element.159.dq_ref, bf16[1024,512]{1,0:T(8,128)(2,1)S(1)} %get-tuple-element.160.dkv_ref, ...), custom_call_target="tpu_custom_call" | custom-call | flops 2617245696 | bytes 7864320 | tf_op jit(solution)/shard_map/qkv_back/pallas_call | solution.py:670
  195.2 3.1 %collective-permute-done.35 = bf16[2,192,1536]{2,1,0:T(8,128)(2,1)S(1)} collective-permute-done((bf16[2,192,1536]{2,1,0:T(8,128)(2,1)}, bf16[2,192,1536]{2,1,0:T(8,128)(2,1)S(1)}, u32[]{:S(2)}, u32[]{:S(2)}) %collective-permute-start.35) | collective-permute-done | bytes 1179680 | tf_op jit(solution)/shard_map/ppermute | solution.py:716
  200.5 2.3 collective-permute-start.39
  202.9 14.4 %attend_back.3 = (bf16[1024,256]{1,0:T(8,128)(2,1)S(1)}, bf16[1024,512]{1,0:T(8,128)(2,1)S(1)}) custom-call(s32[1]{0:T(128)} %constant.169.clone.1.quarter_ref, bf16[1024,512]{1,0:T(8,128)(2,1)S(1)} %copy-done.35, bf16[1024,1024]{1,0:T(8,128)(2,1)S(1)} %copy-done.32, bf16[512,768]{1,0:T(8,128)(2,1)} %get-tuple-element.155.own_ref, ...), custom_call_target="tpu_custom_call" | custom-call | flops 10737418240 | bytes 7864320 | tf_op jit(solution)/shard_map/attend_back/pallas_call | solution.py:326
  217.3 1.6 collective-permute-start.42
  218.8 1.3 collective-permute-start.45
  221.2 3.9 %qkv_back.3 = (f32[512,768]{1,0:T(8,128)S(1)}, bf16[512,768]{1,0:T(8,128)(2,1)S(1)}, bf16[2,192,896]{2,1,0:T(8,128)(2,1)S(1)}, bf16[192,896]{1,0:T(8,128)(2,1)S(1)}, bf16[192,896]{1,0:T(8,128)(2,1)S(1)}) custom-call(bf16[1024,256]{1,0:T(8,128)(2,1)S(1)} %get-tuple-element.174.dq_ref, bf16[1024,512]{1,0:T(8,128)(2,1)S(1)} %get-tuple-element.175.dkv_ref, ...), custom_call_target="tpu_custom_call" | custom-call | flops 2617245696 | bytes 7864320 | tf_op jit(solution)/shard_map/qkv_back/pallas_call | solution.py:670
  226.3 1.3 collective-permute-start.41
  227.5 6.0 %collective-permute-done.49 = bf16[192,1536]{1,0:T(8,128)(2,1)S(1)} collective-permute-done((bf16[192,1536]{1,0:T(8,128)(2,1)S(1)}, bf16[192,1536]{1,0:T(8,128)(2,1)S(1)}, u32[]{:S(2)}, u32[]{:S(2)}) %collective-permute-start.49) | collective-permute-done | bytes 589856 | tf_op jit(solution)/shard_map/ppermute | solution.py:716
  237.3 1.3 collective-permute-start.46
  238.6 8.4 %collective-permute-done.50 = bf16[96,1536]{1,0:T(8,128)(2,1)S(1)} collective-permute-done((bf16[96,1536]{1,0:T(8,128)(2,1)S(1)}, bf16[96,1536]{1,0:T(8,128)(2,1)S(1)}, u32[]{:S(2)}, u32[]{:S(2)}) %collective-permute-start.50) | collective-permute-done | bytes 294944 | tf_op jit(solution)/shard_map/ppermute | solution.py:716
  247.5 1.3 copy.36
  250.2 6.3 %collective-permute-done.47 = bf16[192,896]{1,0:T(8,128)(2,1)S(1)} collective-permute-done((bf16[192,896]{1,0:T(8,128)(2,1)S(1)}, bf16[192,896]{1,0:T(8,128)(2,1)S(1)}, u32[]{:S(2)}, u32[]{:S(2)}) %collective-permute-start.47) | collective-permute-done | bytes 344096 | tf_op jit(solution)/shard_map/ppermute | solution.py:716
  256.7 2.2 collective-permute-done.44
  258.9 1.5 collective-permute-start.51
  261.7 6.3 %collective-permute-done.51 = bf16[96,896]{1,0:T(8,128)(2,1)S(1)} collective-permute-done((bf16[96,896]{1,0:T(8,128)(2,1)S(1)}, bf16[96,896]{1,0:T(8,128)(2,1)S(1)}, u32[]{:S(2)}, u32[]{:S(2)}) %collective-permute-start.51) | collective-permute-done | bytes 172064 | tf_op jit(solution)/shard_map/ppermute | solution.py:716
  (260 shorter events, 54.3 us)
Async XLA Ops:
  2.6 12.9 %collective-permute-start.1 = (bf16[96,768]{1,0:T(8,128)(2,1)S(1)}, bf16[96,768]{1,0:T(8,128)(2,1)S(1)}, u32[]{:S(2)}, u32[]{:S(2)}) collective-permute-start(bf16[96,768]{1,0:T(8,128)(2,1)S(1)} %concatenate.57), channel_id=1, source_target_pairs={{0,16},{1,17},{2,18},{3,19},{4,20},{5,21},{6,22},{7,23},{8,24},{9,... | collective-permute-start | bytes 442376 | tf_op jit(solution)/shard_map/ppermute | solution.py:716
  7.6 6.7 %collective-permute-start.7 = (s32[2,256]{1,0:T(2,128)S(1)}, s32[2,256]{1,0:T(2,128)S(1)}, u32[]{:S(2)}, u32[]{:S(2)}) collective-permute-start(s32[2,256]{1,0:T(2,128)S(1)} %bitcast.105), channel_id=1, source_target_pairs={{0,2},{1,3},{2,0},{3,1},{4,6},{5,7},{6,4},{7,5},{8,10},{9,11},{10,... | collective-permute-start | bytes 6152 | tf_op jit(solution)/shard_map/ppermute | solution.py:716
  11.4 25.3 %collective-permute-start = (bf16[256,768]{1,0:T(8,128)(2,1)S(1)}, bf16[256,768]{1,0:T(8,128)(2,1)S(1)}, u32[]{:S(2)}, u32[]{:S(2)}) collective-permute-start(bf16[256,768]{1,0:T(8,128)(2,1)S(1)} %get-tuple-element.100), channel_id=1, source_target_pairs={{0,2},{1,3},{2,0},{3,1},{4,6},{5,7},{6,4},{7,5},{8,10},{9,11},{10,... | collective-permute-start | bytes 1179656 | tf_op jit(solution)/shard_map/ppermute | solution.py:716
  11.9 41.8 %collective-permute-start.9 = (bf16[256,768]{1,0:T(8,128)(2,1)}, bf16[256,768]{1,0:T(8,128)(2,1)S(1)}, u32[]{:S(2)}, u32[]{:S(2)}) collective-permute-start(bf16[256,768]{1,0:T(8,128)(2,1)} %get-tuple-element.103), channel_id=1, source_target_pairs={{0,2},{1,3},{2,0},{3,1},{4,6},{5,7},{6,4},{7,5},{8,10},{9,11},{10,... | collective-permute-start | bytes 1179656 | tf_op jit(solution)/shard_map/ppermute | solution.py:716
  15.5 11.2 %collective-permute-start.4 = (bf16[192,768]{1,0:T(8,128)(2,1)S(1)}, bf16[192,768]{1,0:T(8,128)(2,1)S(1)}, u32[]{:S(2)}, u32[]{:S(2)}) collective-permute-start(bf16[192,768]{1,0:T(8,128)(2,1)S(1)} %pad_maximum_fusion.9), channel_id=1, source_target_pairs={{0,8},{1,9},{2,10},{3,11},{4,12},{5,13},{6,14},{7,15},{8,0},{9,1},... | collective-permute-start | bytes 884744 | tf_op jit(solution)/shard_map/ppermute | solution.py:716
  19.1 17.2 %collective-permute-start.2 = (bf16[96,1664]{1,0:T(8,128)(2,1)S(1)}, bf16[96,1664]{1,0:T(8,128)(2,1)S(1)}, u32[]{:S(2)}, u32[]{:S(2)}) collective-permute-start(bf16[96,1664]{1,0:T(8,128)(2,1)S(1)} %fusion.43), channel_id=1, source_target_pairs={{0,16},{1,17},{2,18},{3,19},{4,20},{5,21},{6,22},{7,23},{8,24},{9,... | collective-permute-start | bytes 958472 | tf_op jit(solution)/shard_map/ppermute | solution.py:716
  26.8 15.9 %collective-permute-start.5 = (bf16[384,768]{1,0:T(8,128)(2,1)S(1)}, bf16[384,768]{1,0:T(8,128)(2,1)S(1)}, u32[]{:S(2)}, u32[]{:S(2)}) collective-permute-start(bf16[384,768]{1,0:T(8,128)(2,1)S(1)} %pad_maximum_fusion.6.rest_0_.top_ref), channel_id=1, source_target_pairs={{0,2},{1,3},{2,0},{3,1},{4,6},{5,7},{6,4},{7,5},{8,10},{9,11},{10,... | collective-permute-start | bytes 1769480 | tf_op jit(solution)/shard_map/ppermute | solution.py:716
  28.4 14.4 %collective-permute-start.6 = (bf16[384,768]{1,0:T(8,128)(2,1)S(1)}, bf16[384,768]{1,0:T(8,128)(2,1)S(1)}, u32[]{:S(2)}, u32[]{:S(2)}) collective-permute-start(bf16[384,768]{1,0:T(8,128)(2,1)S(1)} %pad_maximum_fusion.6.rest_0_.top_ref), channel_id=1, source_target_pairs={{0,4},{1,5},{2,6},{3,7},{4,0},{5,1},{6,2},{7,3},{8,12},{9,13},{10,... | collective-permute-start | bytes 1769480 | tf_op jit(solution)/shard_map/ppermute | solution.py:716
  36.3 15.4 %collective-permute-start.3 = (bf16[192,1664]{1,0:T(8,128)(2,1)S(1)}, bf16[192,1664]{1,0:T(8,128)(2,1)S(1)}, u32[]{:S(2)}, u32[]{:S(2)}) collective-permute-start(bf16[192,1664]{1,0:T(8,128)(2,1)S(1)} %pad_maximum_fusion.5), channel_id=1, source_target_pairs={{0,8},{1,9},{2,10},{3,11},{4,12},{5,13},{6,14},{7,15},{8,0},{9,1},... | collective-permute-start | bytes 1916936 | tf_op jit(solution)/shard_map/ppermute | solution.py:716
  37.5 22.4 %collective-permute-start.10 = (bf16[512,768]{1,0:T(8,128)(2,1)S(1)}, bf16[512,768]{1,0:T(8,128)(2,1)S(1)}, u32[]{:S(2)}, u32[]{:S(2)}) collective-permute-start(bf16[512,768]{1,0:T(8,128)(2,1)S(1)} %fusion.9.own_ref.x_ref), channel_id=1, source_target_pairs={{0,1},{1,0},{2,3},{3,2},{4,5},{5,4},{6,7},{7,6},{8,9},{9,8},{10,11... | collective-permute-start | bytes 2359304 | tf_op jit(solution)/shard_map/ppermute | solution.py:716
  42.8 17.1 %collective-permute-start.11 = (bf16[384,768]{1,0:T(8,128)(2,1)S(1)}, bf16[384,768]{1,0:T(8,128)(2,1)S(1)}, u32[]{:S(2)}, u32[]{:S(2)}) collective-permute-start(bf16[384,768]{1,0:T(8,128)(2,1)S(1)} %broadcast_select_fusion.2), channel_id=1, source_target_pairs={{0,2},{1,5},{2,0},{3,7},{4,6},{5,1},{6,4},{7,3},{8,10},{9,13},{10,... | collective-permute-start | bytes 1769480 | tf_op jit(solution)/shard_map/ppermute | solution.py:716
  51.9 8.0 %collective-permute-start.14 = (bf16[96,768]{1,0:T(8,128)(2,1)S(1)}, bf16[96,768]{1,0:T(8,128)(2,1)S(1)}, u32[]{:S(2)}, u32[]{:S(2)}) collective-permute-start(bf16[96,768]{1,0:T(8,128)(2,1)S(1)} %pad_maximum_fusion.12), channel_id=1, source_target_pairs={{0,16},{1,17},{2,18},{3,19},{4,20},{5,21},{6,22},{7,23},{8,24},{9,... | collective-permute-start | bytes 442376 | tf_op jit(solution)/shard_map/ppermute | solution.py:716
  52.1 28.8 %collective-permute-start.12 = (bf16[384,1664]{1,0:T(8,128)(2,1)S(1)}, bf16[384,1664]{1,0:T(8,128)(2,1)S(1)}, u32[]{:S(2)}, u32[]{:S(2)}) collective-permute-start(bf16[384,1664]{1,0:T(8,128)(2,1)S(1)} %pad_maximum_fusion.2.norm_a_ref.rest_0_.rest_10_), channel_id=1, source_target_pairs={{0,4},{1,5},{2,6},{3,7},{4,0},{5,1},{6,2},{7,3},{8,12},{9,13},{10,... | collective-permute-start | bytes 3833864 | tf_op jit(solution)/shard_map/ppermute | solution.py:716
  53.6 27.8 %collective-permute-start.13 = (bf16[384,1664]{1,0:T(8,128)(2,1)S(1)}, bf16[384,1664]{1,0:T(8,128)(2,1)S(1)}, u32[]{:S(2)}, u32[]{:S(2)}) collective-permute-start(bf16[384,1664]{1,0:T(8,128)(2,1)S(1)} %pad_maximum_fusion.2.norm_a_ref.rest_0_.rest_10_), channel_id=1, source_target_pairs={{0,2},{1,3},{2,0},{3,1},{4,6},{5,7},{6,4},{7,5},{8,10},{9,11},{10,... | collective-permute-start | bytes 3833864 | tf_op jit(solution)/shard_map/ppermute | solution.py:716
  72.9 8.0 %collective-permute-start.15 = (bf16[192,768]{1,0:T(8,128)(2,1)S(1)}, bf16[192,768]{1,0:T(8,128)(2,1)S(1)}, u32[]{:S(2)}, u32[]{:S(2)}) collective-permute-start(bf16[192,768]{1,0:T(8,128)(2,1)S(1)} %pad_maximum_fusion.10), channel_id=1, source_target_pairs={{0,8},{1,9},{2,10},{3,11},{4,12},{5,13},{6,14},{7,15},{8,0},{9,1},... | collective-permute-start | bytes 884744 | tf_op jit(solution)/shard_map/ppermute | solution.py:716
  81.6 23.6 %collective-permute-start.16 = (bf16[384,1664]{1,0:T(8,128)(2,1)S(1)}, bf16[384,1664]{1,0:T(8,128)(2,1)S(1)}, u32[]{:S(2)}, u32[]{:S(2)}) collective-permute-start(bf16[384,1664]{1,0:T(8,128)(2,1)S(1)} %broadcast_select_fusion), channel_id=1, source_target_pairs={{0,2},{1,5},{2,0},{3,7},{4,6},{5,1},{6,4},{7,3},{8,10},{9,13},{10,... | collective-permute-start | bytes 3833864 | tf_op jit(solution)/shard_map/ppermute | solution.py:716
  84.4 4.9 %collective-permute-start.17 = (bf16[768,512]{1,0:T(8,128)(2,1)S(1)}, bf16[768,512]{1,0:T(8,128)(2,1)S(1)}, u32[]{:S(2)}, u32[]{:S(2)}) collective-permute-start(bf16[768,512]{1,0:T(8,128)(2,1)S(1)} %convolution_convert_fusion.x_a_ref), channel_id=1, source_target_pairs={{0,1},{1,0},{2,3},{3,2},{4,5},{5,4},{6,7},{7,6},{8,9},{9,8},{10,11... | collective-permute-start | bytes 2359304 | tf_op jit(solution)/shard_map/ppermute | solution.py:716
  84.5 20.8 %collective-permute-start.18 = (bf16[512,768]{1,0:T(8,128)(2,1)S(1)}, bf16[512,768]{1,0:T(8,128)(2,1)S(1)}, u32[]{:S(2)}, u32[]{:S(2)}) collective-permute-start(bf16[512,768]{1,0:T(8,128)(2,1)S(1)} %get-tuple-element.121), channel_id=1, source_target_pairs={{0,1},{1,0},{2,3},{3,2},{4,5},{5,4},{6,7},{7,6},{8,9},{9,8},{10,11... | collective-permute-start | bytes 2359304 | tf_op jit(solution)/shard_map/ppermute | solution.py:716
  85.7 26.0 %collective-permute-start.21 = (bf16[384,768]{1,0:T(8,128)(2,1)S(1)}, bf16[384,768]{1,0:T(8,128)(2,1)S(1)}, u32[]{:S(2)}, u32[]{:S(2)}) collective-permute-start(bf16[384,768]{1,0:T(8,128)(2,1)S(1)} %pad_maximum_fusion.7.rest_1_.rest_8_), channel_id=1, source_target_pairs={{0,4},{1,5},{2,6},{3,7},{4,0},{5,1},{6,2},{7,3},{8,12},{9,13},{10,... | collective-permute-start | bytes 1769480 | tf_op jit(solution)/shard_map/ppermute | solution.py:716
  86.3 25.4 %collective-permute-start.22 = (bf16[384,768]{1,0:T(8,128)(2,1)S(1)}, bf16[384,768]{1,0:T(8,128)(2,1)S(1)}, u32[]{:S(2)}, u32[]{:S(2)}) collective-permute-start(bf16[384,768]{1,0:T(8,128)(2,1)S(1)} %pad_maximum_fusion.7.rest_1_.rest_8_), channel_id=1, source_target_pairs={{0,2},{1,3},{2,0},{3,1},{4,6},{5,7},{6,4},{7,5},{8,10},{9,11},{10,... | collective-permute-start | bytes 1769480 | tf_op jit(solution)/shard_map/ppermute | solution.py:716
  106.2 6.5 %collective-permute-start.19 = (bf16[512,768]{1,0:T(8,128)(2,1)S(1)}, bf16[512,768]{1,0:T(8,128)(2,1)S(1)}, u32[]{:S(2)}, u32[]{:S(2)}) collective-permute-start(bf16[512,768]{1,0:T(8,128)(2,1)S(1)} %get-tuple-element.133.low_ref), channel_id=1, source_target_pairs={{0,1},{1,0},{2,3},{3,2},{4,5},{5,4},{6,7},{7,6},{8,9},{9,8},{10,11... | collective-permute-start | bytes 2359304 | tf_op jit(solution)/shard_map/ppermute | solution.py:716
  111.8 9.9 %collective-permute-start.23 = (bf16[384,768]{1,0:T(8,128)(2,1)S(1)}, bf16[384,768]{1,0:T(8,128)(2,1)S(1)}, u32[]{:S(2)}, u32[]{:S(2)}) collective-permute-start(bf16[384,768]{1,0:T(8,128)(2,1)S(1)} %broadcast_select_fusion.1), channel_id=1, source_target_pairs={{0,2},{1,5},{2,0},{3,7},{4,6},{5,1},{6,4},{7,3},{8,10},{9,13},{10,... | collective-permute-start | bytes 1769480 | tf_op jit(solution)/shard_map/ppermute | solution.py:716
  128.5 3.1 %collective-permute-start.25 = (bf16[512,768]{1,0:T(8,128)(2,1)S(1)}, bf16[512,768]{1,0:T(8,128)(2,1)S(1)}, u32[]{:S(2)}, u32[]{:S(2)}) collective-permute-start(bf16[512,768]{1,0:T(8,128)(2,1)S(1)} %get-tuple-element.137.rest_0_), channel_id=1, source_target_pairs={{0,1},{1,0},{2,3},{3,2},{4,5},{5,4},{6,7},{7,6},{8,9},{9,8},{10,11... | collective-permute-start | bytes 2359304 | tf_op jit(solution)/shard_map/ppermute | solution.py:716
  129.0 3.0 %collective-permute-start.26 = (bf16[768,512]{1,0:T(8,128)(2,1)S(1)}, bf16[768,512]{1,0:T(8,128)(2,1)S(1)}, u32[]{:S(2)}, u32[]{:S(2)}) collective-permute-start(bf16[768,512]{1,0:T(8,128)(2,1)S(1)} %get-tuple-element.138.rest_2_), channel_id=1, source_target_pairs={{0,1},{1,0},{2,3},{3,2},{4,5},{5,4},{6,7},{7,6},{8,9},{9,8},{10,11... | collective-permute-start | bytes 2359304 | tf_op jit(solution)/shard_map/ppermute | solution.py:716
  130.8 11.5 %collective-permute-start.27 = (bf16[256,768]{1,0:T(8,128)(2,1)S(1)}, bf16[256,768]{1,0:T(8,128)(2,1)S(1)}, u32[]{:S(2)}, u32[]{:S(2)}) collective-permute-start(bf16[256,768]{1,0:T(8,128)(2,1)S(1)} %get-tuple-element.217), channel_id=1, source_target_pairs={{0,2},{1,3},{2,0},{3,1},{4,6},{5,7},{6,4},{7,5},{8,10},{9,11},{10,... | collective-permute-start | bytes 1179656 | tf_op jit(solution)/shard_map/ppermute | solution.py:716
  140.1 16.9 %collective-permute-start.29 = (bf16[2,192,768]{2,1,0:T(8,128)(2,1)S(1)}, bf16[2,192,768]{2,1,0:T(8,128)(2,1)S(1)}, u32[]{:S(2)}, u32[]{:S(2)}) collective-permute-start(bf16[2,192,768]{2,1,0:T(8,128)(2,1)S(1)} %get-tuple-element.150), channel_id=1, source_target_pairs={{0,4},{1,5},{2,6},{3,7},{4,0},{5,1},{6,2},{7,3},{8,12},{9,13},{10,... | collective-permute-start | bytes 1769480 | tf_op jit(solution)/shard_map/ppermute | solution.py:716
  142.2 14.9 %collective-permute-start.28 = (bf16[2,192,768]{2,1,0:T(8,128)(2,1)S(1)}, bf16[2,192,768]{2,1,0:T(8,128)(2,1)S(1)}, u32[]{:S(2)}, u32[]{:S(2)}) collective-permute-start(bf16[2,192,768]{2,1,0:T(8,128)(2,1)S(1)} %get-tuple-element.149), channel_id=1, source_target_pairs={{0,2},{1,3},{2,0},{3,1},{4,6},{5,7},{6,4},{7,5},{8,10},{9,11},{10,... | collective-permute-start | bytes 1769480 | tf_op jit(solution)/shard_map/ppermute | solution.py:716
  162.4 4.2 %collective-permute-start.31 = (bf16[512,768]{1,0:T(8,128)(2,1)}, bf16[512,768]{1,0:T(8,128)(2,1)}, u32[]{:S(2)}, u32[]{:S(2)}) collective-permute-start(bf16[512,768]{1,0:T(8,128)(2,1)} %get-tuple-element.155.own_ref), channel_id=1, source_target_pairs={{0,1},{1,0},{2,3},{3,2},{4,5},{5,4},{6,7},{7,6},{8,9},{9,8},{10,11... | collective-permute-start | bytes 2359304 | tf_op jit(solution)/shard_map/ppermute | solution.py:716
  162.6 26.7 %collective-permute-start.32 = (bf16[192,768]{1,0:T(8,128)(2,1)}, bf16[192,768]{1,0:T(8,128)(2,1)S(1)}, u32[]{:S(2)}, u32[]{:S(2)}) collective-permute-start(bf16[192,768]{1,0:T(8,128)(2,1)} %get-tuple-element.212), channel_id=1, source_target_pairs={{0,2},{1,3},{2,0},{3,1},{4,6},{5,7},{6,4},{7,5},{8,10},{9,11},{10,... | collective-permute-start | bytes 884744 | tf_op jit(solution)/shard_map/ppermute | solution.py:716
  163.8 36.6 %collective-permute-start.37 = (bf16[192,768]{1,0:T(8,128)(2,1)}, bf16[192,768]{1,0:T(8,128)(2,1)S(1)}, u32[]{:S(2)}, u32[]{:S(2)}) collective-permute-start(bf16[192,768]{1,0:T(8,128)(2,1)} %get-tuple-element.213), channel_id=1, source_target_pairs={{0,4},{1,5},{2,6},{3,7},{4,0},{5,1},{6,2},{7,3},{8,12},{9,13},{10,... | collective-permute-start | bytes 884744 | tf_op jit(solution)/shard_map/ppermute | solution.py:716
  164.7 33.6 %collective-permute-start.35 = (bf16[2,192,1536]{2,1,0:T(8,128)(2,1)}, bf16[2,192,1536]{2,1,0:T(8,128)(2,1)S(1)}, u32[]{:S(2)}, u32[]{:S(2)}) collective-permute-start(bf16[2,192,1536]{2,1,0:T(8,128)(2,1)} %copy-done.26), channel_id=1, source_target_pairs={{0,4},{1,5},{2,6},{3,7},{4,0},{5,1},{6,2},{7,3},{8,12},{9,13},{10,... | collective-permute-start | bytes 3538952 | tf_op jit(solution)/shard_map/ppermute | solution.py:716
  165.8 32.5 %collective-permute-start.34 = (bf16[2,192,1536]{2,1,0:T(8,128)(2,1)}, bf16[2,192,1536]{2,1,0:T(8,128)(2,1)S(1)}, u32[]{:S(2)}, u32[]{:S(2)}) collective-permute-start(bf16[2,192,1536]{2,1,0:T(8,128)(2,1)} %copy-done.25), channel_id=1, source_target_pairs={{0,2},{1,3},{2,0},{3,1},{4,6},{5,7},{6,4},{7,5},{8,10},{9,11},{10,... | collective-permute-start | bytes 3538952 | tf_op jit(solution)/shard_map/ppermute | solution.py:716
  166.7 24.3 %collective-permute-start.33 = (bf16[768,640]{1,0:T(8,128)(2,1)S(1)}, bf16[768,640]{1,0:T(8,128)(2,1)S(1)}, u32[]{:S(2)}, u32[]{:S(2)}) collective-permute-start(bf16[768,640]{1,0:T(8,128)(2,1)S(1)} %get-tuple-element.161.low_a_ref.cols_a_ref), channel_id=1, source_target_pairs={{0,1},{1,0},{2,3},{3,2},{4,5},{5,4},{6,7},{7,6},{8,9},{9,8},{10,11... | collective-permute-start | bytes 2949128 | tf_op jit(solution)/shard_map/ppermute | solution.py:716
  189.4 10.9 %collective-permute-start.38 = (bf16[192,768]{1,0:T(8,128)(2,1)S(1)}, bf16[192,768]{1,0:T(8,128)(2,1)S(1)}, u32[]{:S(2)}, u32[]{:S(2)}) collective-permute-start(bf16[192,768]{1,0:T(8,128)(2,1)S(1)} %fusion.34), channel_id=1, source_target_pairs={{0,8},{1,9},{2,10},{3,11},{4,12},{5,13},{6,14},{7,15},{8,0},{9,1},... | collective-permute-start | bytes 884744 | tf_op jit(solution)/shard_map/ppermute | solution.py:716
  198.6 21.6 %collective-permute-start.36 = (bf16[192,1536]{1,0:T(8,128)(2,1)S(1)}, bf16[192,1536]{1,0:T(8,128)(2,1)S(1)}, u32[]{:S(2)}, u32[]{:S(2)}) collective-permute-start(bf16[192,1536]{1,0:T(8,128)(2,1)S(1)} %get-tuple-element.208), channel_id=1, source_target_pairs={{0,2},{1,3},{2,0},{3,1},{4,6},{5,7},{6,4},{7,5},{8,10},{9,11},{10,... | collective-permute-start | bytes 1769480 | tf_op jit(solution)/shard_map/ppermute | solution.py:716
  199.5 26.7 %collective-permute-start.48 = (bf16[192,1536]{1,0:T(8,128)(2,1)S(1)}, bf16[192,1536]{1,0:T(8,128)(2,1)S(1)}, u32[]{:S(2)}, u32[]{:S(2)}) collective-permute-start(bf16[192,1536]{1,0:T(8,128)(2,1)S(1)} %get-tuple-element.209), channel_id=1, source_target_pairs={{0,4},{1,5},{2,6},{3,7},{4,0},{5,1},{6,2},{7,3},{8,12},{9,13},{10,... | collective-permute-start | bytes 1769480 | tf_op jit(solution)/shard_map/ppermute | solution.py:716
  200.5 19.6 %collective-permute-start.39 = (bf16[96,768]{1,0:T(8,128)(2,1)S(1)}, bf16[96,768]{1,0:T(8,128)(2,1)S(1)}, u32[]{:S(2)}, u32[]{:S(2)}) collective-permute-start(bf16[96,768]{1,0:T(8,128)(2,1)S(1)} %split.41), channel_id=1, source_target_pairs={{0,16},{1,17},{2,18},{3,19},{4,20},{5,21},{6,22},{7,23},{8,24},{9,... | collective-permute-start | bytes 442376 | tf_op jit(solution)/shard_map/ppermute | solution.py:716
  217.3 18.8 %collective-permute-start.42 = (bf16[192,896]{1,0:T(8,128)(2,1)S(1)}, bf16[192,896]{1,0:T(8,128)(2,1)S(1)}, u32[]{:S(2)}, u32[]{:S(2)}) collective-permute-start(bf16[192,896]{1,0:T(8,128)(2,1)S(1)} %get-tuple-element.186), channel_id=1, source_target_pairs={{0,4},{1,5},{2,6},{3,7},{4,0},{5,1},{6,2},{7,3},{8,12},{9,13},{10,... | collective-permute-start | bytes 1032200 | tf_op jit(solution)/shard_map/ppermute | solution.py:716
  218.8 18.4 %collective-permute-start.45 = (bf16[2,192,896]{2,1,0:T(8,128)(2,1)S(1)}, bf16[2,192,896]{2,1,0:T(8,128)(2,1)S(1)}, u32[]{:S(2)}, u32[]{:S(2)}) collective-permute-start(bf16[2,192,896]{2,1,0:T(8,128)(2,1)S(1)} %get-tuple-element.189), channel_id=1, source_target_pairs={{0,2},{1,3},{2,0},{3,1},{4,6},{5,7},{6,4},{7,5},{8,10},{9,11},{10,... | collective-permute-start | bytes 2064392 | tf_op jit(solution)/shard_map/ppermute | solution.py:716
  220.4 13.1 %collective-permute-start.49 = (bf16[192,1536]{1,0:T(8,128)(2,1)S(1)}, bf16[192,1536]{1,0:T(8,128)(2,1)S(1)}, u32[]{:S(2)}, u32[]{:S(2)}) collective-permute-start(bf16[192,1536]{1,0:T(8,128)(2,1)S(1)} %fusion.14), channel_id=1, source_target_pairs={{0,8},{1,9},{2,10},{3,11},{4,12},{5,13},{6,14},{7,15},{8,0},{9,1},... | collective-permute-start | bytes 1769480 | tf_op jit(solution)/shard_map/ppermute | solution.py:716
  225.1 9.2 %collective-permute-start.40 = (bf16[512,768]{1,0:T(8,128)(2,1)S(1)}, bf16[512,768]{1,0:T(8,128)(2,1)S(1)}, u32[]{:S(2)}, u32[]{:S(2)}) collective-permute-start(bf16[512,768]{1,0:T(8,128)(2,1)S(1)} %get-tuple-element.180), channel_id=1, source_target_pairs={{0,1},{1,0},{2,3},{3,2},{4,5},{5,4},{6,7},{7,6},{8,9},{9,8},{10,11... | collective-permute-start | bytes 2359304 | tf_op jit(solution)/shard_map/ppermute | solution.py:716
  226.3 20.9 %collective-permute-start.41 = (bf16[192,896]{1,0:T(8,128)(2,1)S(1)}, bf16[192,896]{1,0:T(8,128)(2,1)S(1)}, u32[]{:S(2)}, u32[]{:S(2)}) collective-permute-start(bf16[192,896]{1,0:T(8,128)(2,1)S(1)} %get-tuple-element.177), channel_id=1, source_target_pairs={{0,4},{1,5},{2,6},{3,7},{4,0},{5,1},{6,2},{7,3},{8,12},{9,13},{10,... | collective-permute-start | bytes 1032200 | tf_op jit(solution)/shard_map/ppermute | solution.py:716
  233.9 13.1 %collective-permute-start.50 = (bf16[96,1536]{1,0:T(8,128)(2,1)S(1)}, bf16[96,1536]{1,0:T(8,128)(2,1)S(1)}, u32[]{:S(2)}, u32[]{:S(2)}) collective-permute-start(bf16[96,1536]{1,0:T(8,128)(2,1)S(1)} %split.39), channel_id=1, source_target_pairs={{0,16},{1,17},{2,18},{3,19},{4,20},{5,21},{6,22},{7,23},{8,24},{9,... | collective-permute-start | bytes 884744 | tf_op jit(solution)/shard_map/ppermute | solution.py:716
  236.3 10.9 %collective-permute-start.43 = (bf16[192,896]{1,0:T(8,128)(2,1)S(1)}, bf16[192,896]{1,0:T(8,128)(2,1)S(1)}, u32[]{:S(2)}, u32[]{:S(2)}) collective-permute-start(bf16[192,896]{1,0:T(8,128)(2,1)S(1)} %add_convert_fusion.3), channel_id=1, source_target_pairs={{0,2},{1,3},{2,0},{3,1},{4,6},{5,7},{6,4},{7,5},{8,10},{9,11},{10,... | collective-permute-start | bytes 1032200 | tf_op jit(solution)/shard_map/ppermute | solution.py:716
  237.3 12.9 %collective-permute-start.46 = (bf16[192,896]{1,0:T(8,128)(2,1)S(1)}, bf16[192,896]{1,0:T(8,128)(2,1)S(1)}, u32[]{:S(2)}, u32[]{:S(2)}) collective-permute-start(bf16[192,896]{1,0:T(8,128)(2,1)S(1)} %fusion.27), channel_id=1, source_target_pairs={{0,4},{1,5},{2,6},{3,7},{4,0},{5,1},{6,2},{7,3},{8,12},{9,13},{10,... | collective-permute-start | bytes 1032200 | tf_op jit(solution)/shard_map/ppermute | solution.py:716
  247.3 9.2 %collective-permute-start.47 = (bf16[192,896]{1,0:T(8,128)(2,1)S(1)}, bf16[192,896]{1,0:T(8,128)(2,1)S(1)}, u32[]{:S(2)}, u32[]{:S(2)}) collective-permute-start(bf16[192,896]{1,0:T(8,128)(2,1)S(1)} %add_convert_fusion.2), channel_id=1, source_target_pairs={{0,8},{1,9},{2,10},{3,11},{4,12},{5,13},{6,14},{7,15},{8,0},{9,1},... | collective-permute-start | bytes 1032200 | tf_op jit(solution)/shard_map/ppermute | solution.py:716
  248.7 10.2 %collective-permute-start.44 = (bf16[256,768]{1,0:T(8,128)(2,1)S(1)}, bf16[256,768]{1,0:T(8,128)(2,1)S(1)}, u32[]{:S(2)}, u32[]{:S(2)}) collective-permute-start(bf16[256,768]{1,0:T(8,128)(2,1)S(1)} %slice.287), channel_id=1, source_target_pairs={{0,2},{1,3},{2,0},{3,1},{4,6},{5,7},{6,4},{7,5},{8,10},{9,11},{10,... | collective-permute-start | bytes 1179656 | tf_op jit(solution)/shard_map/ppermute | solution.py:716
  258.9 9.1 %collective-permute-start.51 = (bf16[96,896]{1,0:T(8,128)(2,1)S(1)}, bf16[96,896]{1,0:T(8,128)(2,1)S(1)}, u32[]{:S(2)}, u32[]{:S(2)}) collective-permute-start(bf16[96,896]{1,0:T(8,128)(2,1)S(1)} %split.40), channel_id=1, source_target_pairs={{0,16},{1,17},{2,18},{3,19},{4,20},{5,21},{6,22},{7,23},{8,24},{9,... | collective-permute-start | bytes 516104 | tf_op jit(solution)/shard_map/ppermute | solution.py:716
  (54 other events, 417.0 us)
